TPU v7x, 1024 devices: a whole 4x8x16 slice. The times are simulated.
1024 devices in a mesh: tm: 8 (over y), band: 8 (over z_hi, core), space: 16 (over z_lo, x).
Axes of the slice: x: 4, y: 8, z: 16 (z_hi: 4, z_lo: 4; z = z_hi * 4 + z_lo), core: 2. Of those that a mesh axis runs over, the one named last changes fastest.
Arguments:
- evecs: bfloat16 [8, 2, 3, 21504, 128], P(None, None, None, ('tm', 'space')), may hold values from -0.31640625 to 0.31640625
- peram: bfloat16 [8, 32, 2, 128, 128], P('tm'), may hold values from -0.375 to 0.375
- mom: int32 [8, 3], P('band'), may hold values from 1 to 2
- pairs: int32 [8, 6], P('band'), may hold values from 0 to 31, as said below
- counts: int32 [8], P('band'), may hold values from 2 to 6, as said below
Outputs:
- meson: float32 [8, 128, 8, 256], P('tm', 'space', 'band')
- blocks: float32 [8, 48, 128, 8, 256], P('tm', 'band', 'space')
Inputs may be any that keep to these rules, and one draw needn't show every extreme that they name: `pairs`: in row b the slots 0 to counts[b] - 1 hold distinct blocks; the other slots hold 0. A block may stand in live slots of several rows. `counts`: the largest count is exactly 6.
All inputs are finite; a program needn't handle non-finite values.
Results may differ from a plain program's by a relative error of at most 0.004.
Values may be sent and summed in bfloat16 or wider, within the bound.
No kernel may reach another device: no remote copies, remote signals or barrier semaphores. Data moves between devices by JAX's collectives and lax.ppermute only.
A program may use at most 32 MiB of HBM per device.

v0:
```python
import math

import jax
import jax.numpy as jnp
from jax import lax
from jax.sharding import PartitionSpec as P

EXTENT = 64


def gram_terms(vectors, momenta, glob):
    tcount = vectors.shape[0]
    sites = vectors.shape[3]
    nvec = vectors.shape[4]
    xs = glob % EXTENT
    ys = glob // EXTENT % EXTENT
    zs = glob // (EXTENT * EXTENT)
    left = vectors.reshape(tcount, 6 * sites, nvec)
    vreal = vectors[:, 0].astype(jnp.float32)
    vimag = vectors[:, 1].astype(jnp.float32)
    row = momenta[0]
    wave = (row[0] * xs + row[1] * ys + row[2] * zs) % EXTENT
    theta = wave.astype(jnp.float32) * jnp.float32(2.0 * math.pi / EXTENT)
    cosine = jnp.cos(theta)[None, None, :, None]
    sine = jnp.sin(theta)[None, None, :, None]
    wreal = cosine * vreal + sine * vimag
    wimag = cosine * vimag - sine * vreal
    right = jnp.stack(
        [jnp.concatenate([wreal, wimag], -1), jnp.concatenate([wimag, -wreal], -1)], axis=1
    )
    right = right.astype(jnp.bfloat16).reshape(tcount, 6 * sites, 2 * nvec)
    results = [jnp.einsum("tsi,tsj->tij", left, right, preferred_element_type=jnp.float32)]
    return jnp.stack(results, axis=2)


def per_device(evecs, peram, mom, pairs, counts):
    spatial = lax.axis_index("space")
    n_space = lax.axis_size("space")
    nvec = evecs.shape[4]
    piece_len = evecs.shape[3]
    glob = (lax.axis_index("tm") * n_space + spatial) * piece_len + jnp.arange(
        piece_len, dtype=jnp.int32
    )
    terms = gram_terms(evecs, mom, glob)
    flat_terms = terms.reshape(terms.shape[0] * nvec, terms.shape[2], 2 * nvec)
    summed = lax.psum_scatter(flat_terms, ("tm", "space"), scatter_dimension=0, tiled=True)
    meson = summed.reshape(1, nvec // n_space, terms.shape[2], 2 * nvec)
    half = meson.astype(jnp.bfloat16)
    chosen = peram[0][pairs[0]]
    preal = chosen[:, 0]
    pimag = chosen[:, 1]
    right = jnp.concatenate(
        [jnp.concatenate([preal, pimag], -1), jnp.concatenate([-pimag, preal], -1)], axis=1
    )
    slot_count = pairs.shape[1]
    live = (jnp.arange(slot_count, dtype=jnp.int32) < counts[0]).astype(jnp.float32)
    piece = lax.all_gather(half, "band", axis=2, tiled=True)
    row_count = piece.shape[1]
    mom_count = piece.shape[2]
    left = piece.reshape(row_count * mom_count, 2 * nvec)
    prod = jnp.einsum("rk,ckn->crn", left, right, preferred_element_type=jnp.float32)
    prod = prod.reshape(1, slot_count, row_count, mom_count, 2 * nvec)
    blocks = prod * live[None, :, None, None, None]
    return (meson, blocks)


def solution(mesh):
    return jax.shard_map(
        per_device,
        mesh=mesh,
        in_specs=(
            P(None, None, None, ("tm", "space"), None),
            P("tm", None, None, None, None),
            P("band", None),
            P("band", None),
            P("band"),
        ),
        out_specs=(P("tm", "space", "band", None), P("tm", "band", "space", None, None)),
        check_vma=False,
    )
```

profile of v0, /device:TPU:1, one launch (start us, length us, event | category | flops | bytes accessed | tf_op | source)
XLA Modules:
  0.0 1482.3 jit_solution(650347009878878739)
XLA Ops:
  7.2 0.0 copy-start
  7.2 0.0 all-reduce.3.cloned.1.call-start
  7.2 1.5 fusion.28
  8.7 2.0 fusion.23
  10.7 2.4 fusion.3
  13.1 0.4 maximum_bitcast_fusion
  13.5 0.4 pad_maximum_fusion
  13.9 0.0 copy-start.1
  13.9 0.3 copy.16
  14.1 1.3 copy-done.1
  15.4 0.9 fusion.29
  16.3 0.0 copy-start.2
  16.4 2.1 copy.17
  18.5 0.0 all-reduce.3.cloned.1.call-update
  19.1 1.3 dynamic-slice
  21.1 0.0 copy-done.2
  21.1 0.0 copy-done
  21.1 0.6 gather_fusion
  21.8 1341.8 %all-reduce.3.cloned.1.call-done = f32[1024,1,256]{2,1,0:T(1,128)} async-done(((f32[1024,1,256]{2,1,0:T(1,128)}), f32[1024,1,256]{2,1,0:T(1,128)}) %all-reduce.3.cloned.1.call-update) | async-done | bytes 1048592
  1363.6 1.3 fusion.27
  1364.9 109.5 %all_gather.3 = bf16[1,8,8,256]{3,1,0,2:T(8,128)(2,1)S(1)} all-gather(bf16[1,8,1,256]{3,1,0,2:T(8,128)(2,1)S(1)} %copy.20), channel_id=1, replica_groups=mesh['tm'=8,'band'=8,'space'=16] {'band'}, dimensions={2}, use_global_device_ids=true | all-gather | bytes 36864 | tf_op jit(solution)/shard_map/all_gather | solution.py:57
  1474.5 1.0 fusion.4
  (6 shorter events, 0.1 us)
Async XLA Ops:
  7.2 13.9 copy-start
  7.2 1356.4 %all-reduce.3.cloned.1.call-start = ((), (), s32[]{:S(2)}) async-start(), calls=%async_computation | async-start | bytes 2097152
  13.9 1.6 copy-start.1
  16.3 4.7 copy-start.2
Sparse Core Ops, SparseCore 0:
  18.6 1344.9 all-reduce.2
where the time goes:
time: 1480 us
  waiting for transfers between devices  1340 us (91%)
  blocking collectives  110 us (7%)
  between operations  15.5 us (1%)
    unnamed x2, waiting for transfers between devices  1340 us
    all_gather x1, blocking collectives, per_device(): piece = lax.all_gather(half, 'band', axis=2, tiled=True)  110 us
  transfers between devices with their start and end apart: 1, of which 1 were waited for; matrix products, arithmetic and copies ran while one was open for 0% of the time, Pallas kernels for 0%

commit v1 on v0

v1 whole, which is shorter than its diff:
```python
import math

import jax
import jax.numpy as jnp
from jax import lax
from jax.experimental import pallas as pl
from jax.experimental.pallas import tpu as pltpu
from jax.sharding import PartitionSpec as P

EXTENT = 64


def gram_kernel(base_ref, mom_ref, pairs_ref, evecs_ref, peram_ref, out_ref, chosen_ref, cos_ref, sin_ref, sems):
    step = pl.program_id(0)
    slots = chosen_ref.shape[0]
    copies = [
        pltpu.make_async_copy(peram_ref.at[pairs_ref[0, c]], chosen_ref.at[c], sems.at[c])
        for c in range(slots)
    ]

    @pl.when(step == 0)
    def _():
        for copy in copies:
            copy.start()
        site = base_ref[0] + lax.broadcasted_iota(jnp.int32, cos_ref.shape, 0)
        xs = site & (EXTENT - 1)
        ys = (site >> 6) & (EXTENT - 1)
        zs = site >> 12
        wave = (mom_ref[0, 0] * xs + mom_ref[0, 1] * ys + mom_ref[0, 2] * zs) & (EXTENT - 1)
        theta = wave.astype(jnp.float32) * jnp.float32(2.0 * math.pi / EXTENT)
        cos_ref[...] = jnp.cos(theta)
        sin_ref[...] = jnp.sin(theta)

    cosine = cos_ref[...]
    sine = sin_ref[...]
    acc = jnp.zeros(out_ref.shape, jnp.float32)
    for colour in range(evecs_ref.shape[2]):
        real = evecs_ref[0, 0, colour]
        imag = evecs_ref[0, 1, colour]
        vreal = real.astype(jnp.float32)
        vimag = imag.astype(jnp.float32)
        wreal = cosine * vreal + sine * vimag
        wimag = cosine * vimag - sine * vreal
        wreal16 = wreal.astype(jnp.bfloat16)
        wimag16 = wimag.astype(jnp.bfloat16)
        upper = jnp.concatenate([wreal16, wimag16], axis=1)
        lower = jnp.concatenate([wimag16, -wreal16], axis=1)
        dims = (((0,), (0,)), ((), ()))
        acc += lax.dot_general(real, upper, dims, preferred_element_type=jnp.float32)
        acc += lax.dot_general(imag, lower, dims, preferred_element_type=jnp.float32)
    out_ref[...] = acc.astype(out_ref.dtype)

    @pl.when(step == pl.num_programs(0) - 1)
    def _():
        for copy in copies:
            copy.wait()


def sum_kernel(parts_ref, meson_ref, half_ref):
    total = jnp.sum(parts_ref[...].astype(jnp.float32), axis=0)
    half = total.astype(jnp.bfloat16)
    for row in range(total.shape[0]):
        meson_ref[row] = total[row : row + 1]
    for band in range(half_ref.shape[0]):
        half_ref[band] = half


def block_kernel(counts_ref, half_ref, chosen_ref, out_ref):
    moms, rows, width = half_ref.shape
    size = moms * rows
    nvec = width // 2
    per_step = out_ref.shape[0]
    left = half_ref[...].reshape(size, width)
    to = lax.broadcasted_iota(jnp.int32, (size, size), 0)
    frm = lax.broadcasted_iota(jnp.int32, (size, size), 1)
    swap = jnp.where((to // moms == frm % rows) & (to % moms == frm // rows), 1.0, 0.0).astype(jnp.bfloat16)
    left = jnp.dot(swap, left, preferred_element_type=jnp.float32)
    mreal = left[:, :nvec]
    mimag = left[:, nvec:]
    both = jnp.concatenate(
        [jnp.concatenate([mreal, -mimag], axis=1), jnp.concatenate([mimag, mreal], axis=1)], axis=0
    ).astype(jnp.bfloat16)
    for c in range(per_step):
        right = chosen_ref[c].reshape(width, nvec)
        prod = jnp.dot(both, right, preferred_element_type=jnp.float32)
        prod = jnp.where(pl.program_id(0) * per_step + c < counts_ref[0], prod, 0.0)
        out_ref[c, :, :, :nvec] = prod[:size].reshape(rows, moms, nvec)
        out_ref[c, :, :, nvec:] = prod[size:].reshape(rows, moms, nvec)


def per_device(evecs, peram, mom, pairs, counts):
    tcount, _, colours, piece_len, nvec = evecs.shape
    n_tm = lax.axis_size("tm")
    n_space = lax.axis_size("space")
    n_band = lax.axis_size("band")
    slots = pairs.shape[1]
    rows = nvec // n_space
    width = 2 * nvec
    base = ((lax.axis_index("tm") * n_space + lax.axis_index("space")) * piece_len).astype(jnp.int32)
    smem = pl.BlockSpec(memory_space=pltpu.SMEM)
    vmem = pl.BlockSpec(memory_space=pltpu.VMEM)
    hbm = pl.BlockSpec(memory_space=pl.ANY)
    parts, chosen = pl.pallas_call(
        gram_kernel,
        grid=(tcount,),
        in_specs=[
            smem,
            smem,
            smem,
            pl.BlockSpec((1, 2, colours, piece_len, nvec), lambda t: (t, 0, 0, 0, 0)),
            hbm,
        ],
        out_specs=[pl.BlockSpec((nvec, width), lambda t: (t, 0)), hbm],
        out_shape=[
            jax.ShapeDtypeStruct((tcount * nvec, width), jnp.bfloat16),
            jax.ShapeDtypeStruct((slots, 2, nvec, nvec), jnp.bfloat16),
        ],
        scratch_shapes=[
            pltpu.VMEM((piece_len, nvec), jnp.float32),
            pltpu.VMEM((piece_len, nvec), jnp.float32),
            pltpu.SemaphoreType.DMA((slots,)),
        ],
        compiler_params=pltpu.CompilerParams(vmem_limit_bytes=16 << 20),
        name="gram",
    )(base.reshape(1), mom, pairs, evecs, peram[0])
    parts = parts.reshape(n_tm * n_space, rows, width)
    parts = lax.all_to_all(parts, ("tm", "space"), 0, 0, tiled=True)
    meson, half = pl.pallas_call(
        sum_kernel,
        in_specs=[vmem],
        out_specs=[vmem, vmem],
        out_shape=[
            jax.ShapeDtypeStruct((rows, 1, width), jnp.float32),
            jax.ShapeDtypeStruct((n_band, rows, width), jnp.bfloat16),
        ],
        compiler_params=pltpu.CompilerParams(vmem_limit_bytes=8 << 20),
        name="total",
    )(parts)
    half = lax.all_to_all(half, "band", 0, 0, tiled=True)
    per_step = 2 if slots % 2 == 0 else 1
    blocks = pl.pallas_call(
        block_kernel,
        grid=(slots // per_step,),
        in_specs=[
            smem,
            vmem,
            pl.BlockSpec((per_step, 2, nvec, nvec), lambda c: (c, 0, 0, 0)),
        ],
        out_specs=pl.BlockSpec((per_step, rows, n_band, width), lambda c: (c, 0, 0, 0)),
        out_shape=jax.ShapeDtypeStruct((slots, rows, n_band, width), jnp.float32),
        compiler_params=pltpu.CompilerParams(vmem_limit_bytes=8 << 20),
        name="blocks",
    )(counts, half, chosen)
    return meson[None], blocks[None]


def solution(mesh):
    return jax.shard_map(
        per_device,
        mesh=mesh,
        in_specs=(
            P(None, None, None, ("tm", "space"), None),
            P("tm", None, None, None, None),
            P("band", None),
            P("band", None),
            P("band"),
        ),
        out_specs=(P("tm", "space", "band", None), P("tm", "band", "space", None, None)),
        check_vma=False,
    )
```

time: 1480 us -> 79.2 us (0.05)
  waiting for transfers between devices: 1340 us -> 11.4 us
  blocking collectives: 110 us -> 36.3 us
  starting transfers between devices: 0.04 us -> 18.4 us
    unnamed x2 -> x0, waiting for transfers between devices: 1340 us -> none
    all_gather x1 -> x0, blocking collectives: 110 us -> none  [per_device(): piece = lax.all_gather(half, 'band', axis=2, tiled=True)]
    all_to_all x0 -> x1, blocking collectives: none -> 36.3 us  [per_device(): parts = lax.all_to_all(parts, ('tm', 'space'), 0, 0, tiled=True)]
    all_to_all x0 -> x1, starting transfers between devices: none -> 18.4 us  [per_device(): half = lax.all_to_all(half, 'band', 0, 0, tiled=True)]
where the time goes in v1:
time: 79.2 us; the launch traced here: 78.8 us
  blocking collectives  36.3 us (46%)
  starting transfers between devices  18.4 us (23%)
  waiting for transfers between devices  11.4 us (14%)
  Pallas kernels  7 us (9%)
  local copies, waits for them, and re-layouts  4.47 us (6%)
  between operations  1.31 us (2%)
    all_to_all x1, blocking collectives, per_device(): parts = lax.all_to_all(parts, ('tm', 'space'), 0, 0, tiled=True)  36.3 us
    all_to_all x1, starting transfers between devices, per_device(): half = lax.all_to_all(half, 'band', 0, 0, tiled=True)  18.4 us
    all_to_all x1, waiting for transfers between devices, per_device(): half = lax.all_to_all(half, 'band', 0, 0, tiled=True)  11.4 us
    unnamed x8, local copies, waits for them, and re-layouts  4.47 us
    pallas_call x1, Pallas kernels, per_device(): pl.pallas_call(gram_kernel, grid=(tcount,), in_specs=[smem, smem, smem, p...  4.35 us
    pallas_call x1, Pallas kernels, per_device(): pl.pallas_call(block_kernel, grid=(slots // per_step,), in_specs=[smem, v...  1.89 us
  transfers between devices with their start and end apart: 1, of which 1 were waited for; matrix products, arithmetic and copies ran while one was open for 0% of the time, Pallas kernels for 0%

profile of v1, /device:TPU:1, one launch (start us, length us, event | category | flops | bytes accessed | tf_op | source)
XLA Modules:
  0.0 78.8 jit_solution(17158243245579264404)
XLA Ops:
  0.6 0.0 copy-start
  0.6 1.6 %copy-done = bf16[1,32,2,128,128]{4,3,2,1,0:T(8,128)(2,1)S(1)} copy-done((bf16[1,32,2,128,128]{4,3,2,1,0:T(8,128)(2,1)S(1)}, bf16[1,32,2,128,128]{4,3,2,1,0:T(8,128)(2,1)}, u32[]{:S(2)}) %copy-start) | copy-done | bytes 2097176
  2.2 0.0 copy-start.1
  2.2 1.6 %copy-done.1 = bf16[8,2,3,168,128]{4,3,2,1,0:T(8,128)(2,1)S(1)} copy-done((bf16[8,2,3,168,128]{4,3,2,1,0:T(8,128)(2,1)S(1)}, bf16[8,2,3,168,128]{4,3,2,1,0:T(8,128)(2,1)}, u32[]{:S(2)}) %copy-start.1) | copy-done | bytes 2064408
  3.8 0.0 copy-start.2
  3.8 0.7 copy-done.2
  4.5 0.0 copy-start.3
  4.5 0.7 copy-done.3
  5.1 4.4 %gram.1 = (bf16[1024,256]{1,0:T(8,128)(2,1)S(1)}, bf16[6,2,128,128]{3,2,1,0:T(8,128)(2,1)S(1)}) custom-call(s32[1]{0:T(128)} %bitcast.base_ref, s32[1,3]{1,0:T(1,128)S(1)} %copy-done.2, s32[1,6]{1,0:T(1,128)S(1)} %copy-done.3, bf16[8,2,3,168,128]{4,3,2,1,0:T(8,128)(2,1)S(1)} %copy-done.1, bf16[32,2,128,128]{3,2,1,0:T(8,128)(2,1)S(1)} %bitcast.5), custom_call_target="tpu_custom_call" | custom-call | tf_op jit(solution)/shard_map/gram/pallas_call | solution.py:103
  9.5 36.3 %all_to_all.10.parts_ref = bf16[128,8,256]{2,1,0:T(8,128)(2,1)S(1)} all-to-all(bf16[128,8,256]{2,1,0:T(8,128)(2,1)S(1)} %bitcast.6), channel_id=1, replica_groups=mesh['tm'=8,'band'=8,'space'=16] {'tm','space'}, dimensions={0} | all-to-all | bytes 1048576 | tf_op jit(solution)/shard_map/all_to_all | solution.py:127
  45.8 0.8 total.1
  46.5 18.4 %all-to-all-start.1 = ((bf16[8,8,256]{2,1,0:T(8,128)(2,1)}), bf16[8,8,256]{2,1,0:T(8,128)(2,1)S(1)}, u32[]{:S(2)}, u32[]{:S(2)}) async-start(bf16[8,8,256]{2,1,0:T(8,128)(2,1)} %get-tuple-element.8), calls=%async_computation.1 | async-start | bytes 65536 | tf_op jit(solution)/shard_map/all_to_all | solution.py:139
  65.6 11.4 %all-to-all-done.1.half_ref = bf16[8,8,256]{2,1,0:T(8,128)(2,1)S(1)} async-done(((bf16[8,8,256]{2,1,0:T(8,128)(2,1)}), bf16[8,8,256]{2,1,0:T(8,128)(2,1)S(1)}, u32[]{:S(2)}, u32[]{:S(2)}) %all-to-all-start.1) | async-done | bytes 32800 | tf_op jit(solution)/shard_map/all_to_all | solution.py:139
  77.0 1.9 %blocks.1 = f32[6,8,8,256]{3,2,1,0:T(8,128)} custom-call(s32[1]{0:T(128)S(6)} %copy.7.counts_ref, bf16[8,8,256]{2,1,0:T(8,128)(2,1)S(1)} %all-to-all-done.1.half_ref, bf16[6,2,128,128]{3,2,1,0:T(8,128)(2,1)S(1)} %get-tuple-element.9.chosen_ref), custom_call_target="tpu_custom_call" | custom-call | tf_op jit(solution)/shard_map/blocks/pallas_call | solution.py:141
Async XLA Ops:
  0.6 1.6 %copy-start = (bf16[1,32,2,128,128]{4,3,2,1,0:T(8,128)(2,1)S(1)}, bf16[1,32,2,128,128]{4,3,2,1,0:T(8,128)(2,1)}, u32[]{:S(2)}) copy-start(bf16[1,32,2,128,128]{4,3,2,1,0:T(8,128)(2,1)} %param.6) | copy-start | bytes 6291460
  2.2 1.6 %copy-start.1 = (bf16[8,2,3,168,128]{4,3,2,1,0:T(8,128)(2,1)S(1)}, bf16[8,2,3,168,128]{4,3,2,1,0:T(8,128)(2,1)}, u32[]{:S(2)}) copy-start(bf16[8,2,3,168,128]{4,3,2,1,0:T(8,128)(2,1)} %evecs_ref.1) | copy-start | bytes 6193156
  3.8 0.7 copy-start.2
  4.5 0.7 copy-start.3
  46.5 30.4 %all-to-all-start.1 = ((bf16[8,8,256]{2,1,0:T(8,128)(2,1)}), bf16[8,8,256]{2,1,0:T(8,128)(2,1)S(1)}, u32[]{:S(2)}, u32[]{:S(2)}) async-start(bf16[8,8,256]{2,1,0:T(8,128)(2,1)} %get-tuple-element.8), calls=%async_computation.1 | async-start | bytes 65536 | tf_op jit(solution)/shard_map/all_to_all | solution.py:139

commit v2 on v1

--- a/solution.py
+++ b/solution.py
@@ -10,50 +10,58 @@
 EXTENT = 64
 
 
-def gram_kernel(base_ref, mom_ref, pairs_ref, evecs_ref, peram_ref, out_ref, chosen_ref, cos_ref, sin_ref, sems):
-    step = pl.program_id(0)
+def gram_kernel(
+    base_ref, mom_hbm, pairs_hbm, evecs_hbm, peram_hbm, out_ref, chosen_ref,
+    evecs_ref, right_ref, mom_ref, pairs_ref, evecs_sems, small_sems, pick_sems,
+):
+    tcount, _, colours, sites, nvec = evecs_ref.shape
     slots = chosen_ref.shape[0]
-    copies = [
-        pltpu.make_async_copy(peram_ref.at[pairs_ref[0, c]], chosen_ref.at[c], sems.at[c])
+    small = [
+        pltpu.make_async_copy(mom_hbm, mom_ref, small_sems.at[0]),
+        pltpu.make_async_copy(pairs_hbm, pairs_ref, small_sems.at[1]),
+    ]
+    loads = [
+        pltpu.make_async_copy(evecs_hbm.at[t], evecs_ref.at[t], evecs_sems.at[t]) for t in range(tcount)
+    ]
+    for copy in small + loads:
+        copy.start()
+    site = base_ref[0] + lax.broadcasted_iota(jnp.int32, (sites, nvec), 0)
+    xs = site & (EXTENT - 1)
+    ys = (site >> 6) & (EXTENT - 1)
+    zs = site >> 12
+    for copy in small:
+        copy.wait()
+    picks = [
+        pltpu.make_async_copy(peram_hbm.at[pairs_ref[0, c]], chosen_ref.at[c], pick_sems.at[c])
         for c in range(slots)
     ]
-
-    @pl.when(step == 0)
-    def _():
-        for copy in copies:
-            copy.start()
-        site = base_ref[0] + lax.broadcasted_iota(jnp.int32, cos_ref.shape, 0)
-        xs = site & (EXTENT - 1)
-        ys = (site >> 6) & (EXTENT - 1)
-        zs = site >> 12
-        wave = (mom_ref[0, 0] * xs + mom_ref[0, 1] * ys + mom_ref[0, 2] * zs) & (EXTENT - 1)
-        theta = wave.astype(jnp.float32) * jnp.float32(2.0 * math.pi / EXTENT)
-        cos_ref[...] = jnp.cos(theta)
-        sin_ref[...] = jnp.sin(theta)
-
-    cosine = cos_ref[...]
-    sine = sin_ref[...]
-    acc = jnp.zeros(out_ref.shape, jnp.float32)
-    for colour in range(evecs_ref.shape[2]):
-        real = evecs_ref[0, 0, colour]
-        imag = evecs_ref[0, 1, colour]
-        vreal = real.astype(jnp.float32)
-        vimag = imag.astype(jnp.float32)
-        wreal = cosine * vreal + sine * vimag
-        wimag = cosine * vimag - sine * vreal
-        wreal16 = wreal.astype(jnp.bfloat16)
-        wimag16 = wimag.astype(jnp.bfloat16)
-        upper = jnp.concatenate([wreal16, wimag16], axis=1)
-        lower = jnp.concatenate([wimag16, -wreal16], axis=1)
-        dims = (((0,), (0,)), ((), ()))
-        acc += lax.dot_general(real, upper, dims, preferred_element_type=jnp.float32)
-        acc += lax.dot_general(imag, lower, dims, preferred_element_type=jnp.float32)
-    out_ref[...] = acc.astype(out_ref.dtype)
-
-    @pl.when(step == pl.num_programs(0) - 1)
-    def _():
-        for copy in copies:
-            copy.wait()
+    for copy in picks:
+        copy.start()
+    wave = (mom_ref[0, 0] * xs + mom_ref[0, 1] * ys + mom_ref[0, 2] * zs) & (EXTENT - 1)
+    theta = wave.astype(jnp.float32) * jnp.float32(2.0 * math.pi / EXTENT)
+    cosine = jnp.cos(theta)
+    sine = jnp.sin(theta)
+    for t in range(tcount):
+        loads[t].wait()
+        slot = t % 2
+        for colour in range(colours):
+            vreal = evecs_ref[t, 0, colour].astype(jnp.float32)
+            vimag = evecs_ref[t, 1, colour].astype(jnp.float32)
+            wreal = (cosine * vreal + sine * vimag).astype(jnp.bfloat16)
+            wimag = (cosine * vimag - sine * vreal).astype(jnp.bfloat16)
+            right_ref[slot, 0, colour, :, :nvec] = wreal
+            right_ref[slot, 0, colour, :, nvec:] = wimag
+            right_ref[slot, 1, colour, :, :nvec] = wimag
+            right_ref[slot, 1, colour, :, nvec:] = -wreal
+        acc = lax.dot_general(
+            evecs_ref[t].reshape(2 * colours * sites, nvec),
+            right_ref[slot].reshape(2 * colours * sites, 2 * nvec),
+            (((0,), (0,)), ((), ())),
+            preferred_element_type=jnp.float32,
+        )
+        out_ref[t * nvec : (t + 1) * nvec] = acc.astype(out_ref.dtype)
+    for copy in picks:
+        copy.wait()
 
 
 def sum_kernel(parts_ref, meson_ref, half_ref):
@@ -99,30 +107,27 @@
     base = ((lax.axis_index("tm") * n_space + lax.axis_index("space")) * piece_len).astype(jnp.int32)
     smem = pl.BlockSpec(memory_space=pltpu.SMEM)
     vmem = pl.BlockSpec(memory_space=pltpu.VMEM)
-    hbm = pl.BlockSpec(memory_space=pl.ANY)
+    hbm = pl.BlockSpec(memory_space=pltpu.HBM)
     parts, chosen = pl.pallas_call(
         gram_kernel,
-        grid=(tcount,),
-        in_specs=[
-            smem,
-            smem,
-            smem,
-            pl.BlockSpec((1, 2, colours, piece_len, nvec), lambda t: (t, 0, 0, 0, 0)),
-            hbm,
-        ],
-        out_specs=[pl.BlockSpec((nvec, width), lambda t: (t, 0)), hbm],
+        in_specs=[smem, hbm, hbm, hbm, hbm],
+        out_specs=[vmem, vmem],
         out_shape=[
             jax.ShapeDtypeStruct((tcount * nvec, width), jnp.bfloat16),
             jax.ShapeDtypeStruct((slots, 2, nvec, nvec), jnp.bfloat16),
         ],
         scratch_shapes=[
-            pltpu.VMEM((piece_len, nvec), jnp.float32),
-            pltpu.VMEM((piece_len, nvec), jnp.float32),
+            pltpu.VMEM((tcount, 2, colours, piece_len, nvec), jnp.bfloat16),
+            pltpu.VMEM((2, 2, colours, piece_len, width), jnp.bfloat16),
+            pltpu.SMEM(mom.shape, jnp.int32),
+            pltpu.SMEM(pairs.shape, jnp.int32),
+            pltpu.SemaphoreType.DMA((tcount,)),
+            pltpu.SemaphoreType.DMA((2,)),
             pltpu.SemaphoreType.DMA((slots,)),
         ],
         compiler_params=pltpu.CompilerParams(vmem_limit_bytes=16 << 20),
         name="gram",
-    )(base.reshape(1), mom, pairs, evecs, peram[0])
+    )(base.reshape(1), *(pltpu.with_memory_space_constraint(a, pltpu.HBM) for a in (mom, pairs, evecs, peram[0])))
     parts = parts.reshape(n_tm * n_space, rows, width)
     parts = lax.all_to_all(parts, ("tm", "space"), 0, 0, tiled=True)
     meson, half = pl.pallas_call(

time: 79.2 us -> 74.4 us (0.939)
  local copies, waits for them, and re-layouts: 4.47 us -> 0 us
    unnamed x8 -> x0, local copies, waits for them, and re-layouts: 4.47 us -> none
where the time goes in v2:
time: 74.4 us; the launch traced here: 74.1 us
  blocking collectives  36.3 us (49%)
  starting transfers between devices  18.4 us (25%)
  waiting for transfers between devices  11.4 us (15%)
  Pallas kernels  6.77 us (9%)
  between operations  1.3 us (2%)
    all_to_all x1, blocking collectives, per_device(): parts = lax.all_to_all(parts, ('tm', 'space'), 0, 0, tiled=True)  36.3 us
    all_to_all x1, starting transfers between devices, per_device(): half = lax.all_to_all(half, 'band', 0, 0, tiled=True)  18.4 us
    all_to_all x1, waiting for transfers between devices, per_device(): half = lax.all_to_all(half, 'band', 0, 0, tiled=True)  11.4 us
    pallas_call x1, Pallas kernels, per_device(): pl.pallas_call(gram_kernel, in_specs=[smem, hbm, hbm, hbm, hbm], out_spec...  4.12 us
    pallas_call x1, Pallas kernels, per_device(): pl.pallas_call(block_kernel, grid=(slots // per_step,), in_specs=[smem, v...  1.89 us
  transfers between devices with their start and end apart: 1, of which 1 were waited for; matrix products, arithmetic and copies ran while one was open for 0% of the time, Pallas kernels for 0%

profile of v2, /device:TPU:1, one launch (start us, length us, event | category | flops | bytes accessed | tf_op | source)
XLA Modules:
  0.0 74.1 jit_solution(5937341693027398248)
XLA Ops:
  0.6 4.1 %gram.1 = (bf16[1024,256]{1,0:T(8,128)(2,1)S(1)}, bf16[6,2,128,128]{3,2,1,0:T(8,128)(2,1)S(1)}) custom-call(s32[1]{0:T(128)} %bitcast.base_ref, s32[1,3]{1,0:T(1,128)} %mom_hbm.1, s32[1,6]{1,0:T(1,128)} %pairs_hbm.1, bf16[8,2,3,168,128]{4,3,2,1,0:T(8,128)(2,1)} %evecs_hbm.1, bf16[32,2,128,128]{3,2,1,0:T(8,128)(2,1)} %bitcast.6), custom_call_target="tpu_custom_call" | custom-call | tf_op jit(solution)/shard_map/gram/pallas_call | solution.py:111
  4.8 36.3 %all_to_all.10.parts_ref = bf16[128,8,256]{2,1,0:T(8,128)(2,1)S(1)} all-to-all(bf16[128,8,256]{2,1,0:T(8,128)(2,1)S(1)} %bitcast.5), channel_id=1, replica_groups=mesh['tm'=8,'band'=8,'space'=16] {'tm','space'}, dimensions={0} | all-to-all | bytes 1048576 | tf_op jit(solution)/shard_map/all_to_all | solution.py:132
  41.1 0.8 %total.1 = (f32[8,1,256]{2,1,0:T(1,128)}, bf16[8,8,256]{2,1,0:T(8,128)(2,1)}) custom-call(bf16[128,8,256]{2,1,0:T(8,128)(2,1)S(1)} %all_to_all.10.parts_ref), custom_call_target="tpu_custom_call" | custom-call | tf_op jit(solution)/shard_map/total/pallas_call | solution.py:133
  41.8 18.4 %all-to-all-start.1 = ((bf16[8,8,256]{2,1,0:T(8,128)(2,1)}), bf16[8,8,256]{2,1,0:T(8,128)(2,1)S(1)}, u32[]{:S(2)}, u32[]{:S(2)}) async-start(bf16[8,8,256]{2,1,0:T(8,128)(2,1)} %get-tuple-element.8), calls=%async_computation.1 | async-start | bytes 65536 | tf_op jit(solution)/shard_map/all_to_all | solution.py:144
  60.9 11.4 %all-to-all-done.1.half_ref = bf16[8,8,256]{2,1,0:T(8,128)(2,1)S(1)} async-done(((bf16[8,8,256]{2,1,0:T(8,128)(2,1)}), bf16[8,8,256]{2,1,0:T(8,128)(2,1)S(1)}, u32[]{:S(2)}, u32[]{:S(2)}) %all-to-all-start.1) | async-done | bytes 32800 | tf_op jit(solution)/shard_map/all_to_all | solution.py:144
  72.2 1.9 %blocks.1 = f32[6,8,8,256]{3,2,1,0:T(8,128)} custom-call(s32[1]{0:T(128)S(6)} %copy.7.counts_ref, bf16[8,8,256]{2,1,0:T(8,128)(2,1)S(1)} %all-to-all-done.1.half_ref, bf16[6,2,128,128]{3,2,1,0:T(8,128)(2,1)S(1)} %get-tuple-element.9.chosen_ref), custom_call_target="tpu_custom_call" | custom-call | tf_op jit(solution)/shard_map/blocks/pallas_call | solution.py:146
Async XLA Ops:
  41.8 30.4 %all-to-all-start.1 = ((bf16[8,8,256]{2,1,0:T(8,128)(2,1)}), bf16[8,8,256]{2,1,0:T(8,128)(2,1)S(1)}, u32[]{:S(2)}, u32[]{:S(2)}) async-start(bf16[8,8,256]{2,1,0:T(8,128)(2,1)} %get-tuple-element.8), calls=%async_computation.1 | async-start | bytes 65536 | tf_op jit(solution)/shard_map/all_to_all | solution.py:144

commit v3 on v2

v3 whole, which is shorter than its diff:
```python
import math

import jax
import jax.numpy as jnp
from jax import lax
from jax.experimental import pallas as pl
from jax.experimental.pallas import tpu as pltpu
from jax.sharding import Mesh, PartitionSpec as P

EXTENT = 64
Z_LO = 4


def gram_kernel(
    base_ref, mom_hbm, pairs_hbm, evecs_hbm, peram_hbm, out_ref, chosen_ref,
    evecs_ref, right_ref, mom_ref, pairs_ref, evecs_sems, small_sems, pick_sems,
):
    tcount, _, colours, sites, nvec = evecs_ref.shape
    slots = chosen_ref.shape[0]
    n_x = out_ref.shape[0] // tcount
    n_zl, rows = out_ref.shape[1:3]
    small = [
        pltpu.make_async_copy(mom_hbm, mom_ref, small_sems.at[0]),
        pltpu.make_async_copy(pairs_hbm, pairs_ref, small_sems.at[1]),
    ]
    loads = [
        pltpu.make_async_copy(evecs_hbm.at[t], evecs_ref.at[t], evecs_sems.at[t]) for t in range(tcount)
    ]
    for copy in small + loads:
        copy.start()
    site = base_ref[0] + lax.broadcasted_iota(jnp.int32, (sites, nvec), 0)
    xs = site & (EXTENT - 1)
    ys = (site >> 6) & (EXTENT - 1)
    zs = site >> 12
    for copy in small:
        copy.wait()
    picks = [
        pltpu.make_async_copy(peram_hbm.at[pairs_ref[0, c]], chosen_ref.at[c], pick_sems.at[c])
        for c in range(slots)
    ]
    for copy in picks:
        copy.start()
    wave = (mom_ref[0, 0] * xs + mom_ref[0, 1] * ys + mom_ref[0, 2] * zs) & (EXTENT - 1)
    theta = wave.astype(jnp.float32) * jnp.float32(2.0 * math.pi / EXTENT)
    cosine = jnp.cos(theta)
    sine = jnp.sin(theta)
    for t in range(tcount):
        loads[t].wait()
        slot = t % 2
        for colour in range(colours):
            real = evecs_ref[t, 0, colour]
            imag = evecs_ref[t, 1, colour]
            vreal = real.astype(jnp.float32)
            vimag = imag.astype(jnp.float32)
            right_ref[slot, colour, :, :nvec] = (cosine * vreal + sine * vimag).astype(jnp.bfloat16)
            right_ref[slot, colour, :, nvec:] = (cosine * vimag - sine * vreal).astype(jnp.bfloat16)
        acc = jnp.concatenate([lax.dot_general(
            evecs_ref[t, q].reshape(colours * sites, nvec),
            right_ref[slot].reshape(colours * sites, 2 * nvec),
            (((0,), (0,)), ((), ())),
            preferred_element_type=jnp.float32,
        ) for q in range(2)], axis=0)
        meson = jnp.concatenate(
            [acc[:nvec, :nvec] + acc[nvec:, nvec:], acc[:nvec, nvec:] - acc[nvec:, :nvec]], axis=1
        )
        meson = meson.astype(out_ref.dtype)
        for x in range(n_x):
            for zl in range(n_zl):
                first = (zl * n_x + x) * rows
                out_ref[t * n_x + x, zl] = meson[first : first + rows]
    for copy in picks:
        copy.wait()


def sum_kernel(parts_ref, out_ref):
    total = jnp.sum(parts_ref[...].astype(jnp.float32), axis=0).astype(jnp.bfloat16)
    for band in range(out_ref.shape[0]):
        out_ref[band] = total


def block_kernel(band_ref, counts_ref, parts_ref, chosen_ref, meson_ref, out_hbm, total_ref, out_ref, sems):
    moms, _, rows, width = parts_ref.shape
    slots = out_ref.shape[0]
    size = moms * rows
    nvec = width // 2
    total_ref[...] = jnp.sum(parts_ref[...].astype(jnp.float32), axis=1)
    left = total_ref[...].astype(jnp.bfloat16).reshape(size, width)
    to = lax.broadcasted_iota(jnp.int32, (size, size), 0)
    frm = lax.broadcasted_iota(jnp.int32, (size, size), 1)
    swap = jnp.where((to // moms == frm % rows) & (to % moms == frm // rows), 1.0, 0.0).astype(jnp.bfloat16)
    left = jnp.dot(swap, left, preferred_element_type=jnp.float32)
    mreal = left[:, :nvec]
    mimag = left[:, nvec:]
    both = jnp.concatenate(
        [jnp.concatenate([mreal, -mimag], axis=1), jnp.concatenate([mimag, mreal], axis=1)], axis=0
    ).astype(jnp.bfloat16)
    copies = []
    for c in range(slots):
        right = chosen_ref[c].reshape(width, nvec)
        prod = jnp.dot(both, right, preferred_element_type=jnp.float32)
        prod = jnp.where(c < counts_ref[0], prod, 0.0)
        out_ref[c, :, :, :nvec] = prod[:size].reshape(rows, moms, nvec)
        out_ref[c, :, :, nvec:] = prod[size:].reshape(rows, moms, nvec)
        copies.append(pltpu.make_async_copy(out_ref.at[c], out_hbm.at[c], sems.at[c]))
        copies[-1].start()
    own = total_ref[band_ref[0]]
    for row in range(rows):
        meson_ref[row] = own[row : row + 1]
    for copy in copies:
        copy.wait()


def per_device(evecs, peram, mom, pairs, counts):
    tcount, _, colours, piece_len, nvec = evecs.shape
    n_tm = lax.axis_size("tm")
    n_zl = lax.axis_size("z_lo")
    n_x = lax.axis_size("x")
    n_band = lax.axis_size("band")
    slots = pairs.shape[1]
    rows = nvec // (n_zl * n_x)
    width = 2 * nvec
    place = (lax.axis_index("tm") * n_zl + lax.axis_index("z_lo")) * n_x + lax.axis_index("x")
    base = (place * piece_len).astype(jnp.int32)
    smem = pl.BlockSpec(memory_space=pltpu.SMEM)
    vmem = pl.BlockSpec(memory_space=pltpu.VMEM)
    hbm = pl.BlockSpec(memory_space=pltpu.HBM)
    parts, chosen = pl.pallas_call(
        gram_kernel,
        in_specs=[smem, hbm, hbm, hbm, hbm],
        out_specs=[vmem, vmem],
        out_shape=[
            jax.ShapeDtypeStruct((n_tm * n_x, n_zl, rows, width), jnp.bfloat16),
            jax.ShapeDtypeStruct((slots, 2, nvec, nvec), jnp.bfloat16),
        ],
        scratch_shapes=[
            pltpu.VMEM((tcount, 2, colours, piece_len, nvec), jnp.bfloat16),
            pltpu.VMEM((2, colours, piece_len, width), jnp.bfloat16),
            pltpu.SMEM(mom.shape, jnp.int32),
            pltpu.SMEM(pairs.shape, jnp.int32),
            pltpu.SemaphoreType.DMA((tcount,)),
            pltpu.SemaphoreType.DMA((2,)),
            pltpu.SemaphoreType.DMA((slots,)),
        ],
        compiler_params=pltpu.CompilerParams(vmem_limit_bytes=16 << 20),
        name="gram",
    )(base.reshape(1), *(pltpu.with_memory_space_constraint(a, pltpu.HBM) for a in (mom, pairs, evecs, peram[0])))
    parts = lax.all_to_all(parts, ("tm", "x"), 0, 0, tiled=True)
    parts = pl.pallas_call(
        sum_kernel,
        in_specs=[vmem],
        out_specs=vmem,
        out_shape=jax.ShapeDtypeStruct((n_band, n_zl, rows, width), jnp.bfloat16),
        compiler_params=pltpu.CompilerParams(vmem_limit_bytes=8 << 20),
        name="total",
    )(parts)
    parts = parts.reshape(n_band * n_zl, rows, width)
    parts = lax.all_to_all(parts, ("band", "z_lo"), 0, 0, tiled=True)
    meson, blocks = pl.pallas_call(
        block_kernel,
        in_specs=[smem, smem, vmem, vmem],
        out_specs=[vmem, hbm],
        out_shape=[
            jax.ShapeDtypeStruct((rows, 1, width), jnp.float32),
            jax.ShapeDtypeStruct((slots, rows, n_band, width), jnp.float32),
        ],
        scratch_shapes=[
            pltpu.VMEM((n_band, rows, width), jnp.float32),
            pltpu.VMEM((slots, rows, n_band, width), jnp.float32),
            pltpu.SemaphoreType.DMA((slots,)),
        ],
        compiler_params=pltpu.CompilerParams(vmem_limit_bytes=8 << 20),
        name="blocks",
    )(
        lax.axis_index("band").astype(jnp.int32).reshape(1),
        counts,
        parts.reshape(n_band, n_zl, rows, width),
        chosen,
    )
    return meson[None], blocks[None]


def solution(mesh):
    n_tm, n_band, n_space = (mesh.shape[name] for name in ("tm", "band", "space"))
    fine = Mesh(mesh.devices.reshape(n_tm, n_band, Z_LO, n_space // Z_LO), ("tm", "band", "z_lo", "x"))
    return jax.shard_map(
        per_device,
        mesh=fine,
        in_specs=(
            P(None, None, None, ("tm", "z_lo", "x"), None),
            P("tm", None, None, None, None),
            P("band", None),
            P("band", None),
            P("band"),
        ),
        out_specs=(P("tm", ("z_lo", "x"), "band", None), P("tm", "band", ("z_lo", "x"), None, None)),
        check_vma=False,
    )
```

time: 74.4 us -> 71.1 us (0.956)
  blocking collectives: 36.3 us -> 23 us
  starting transfers between devices: 18.4 us -> 24.9 us
  waiting for transfers between devices: 11.4 us -> 15.4 us
    all_to_all x1, blocking collectives: 36.3 us -> 23 us  [per_device(): parts = lax.all_to_all(parts, ('tm', 'x'), 0, 0, tiled=True)]
    all_to_all x1, starting transfers between devices: 18.4 us -> 24.9 us  [per_device(): parts = lax.all_to_all(parts, ('band', 'z_lo'), 0, 0, tiled=True)]
    all_to_all x1, waiting for transfers between devices: 11.4 us -> 15.4 us  [per_device(): parts = lax.all_to_all(parts, ('band', 'z_lo'), 0, 0, tiled=True)]
where the time goes in v3:
time: 71.1 us; the launch traced here: 70.8 us
  starting transfers between devices  24.9 us (35%)
  blocking collectives  23 us (32%)
  waiting for transfers between devices  15.4 us (22%)
  Pallas kernels  6.25 us (9%)
  between operations  1.31 us (2%)
    all_to_all x1, starting transfers between devices, per_device(): parts = lax.all_to_all(parts, ('band', 'z_lo'), 0, 0, tiled=True)  24.9 us
    all_to_all x1, blocking collectives, per_device(): parts = lax.all_to_all(parts, ('tm', 'x'), 0, 0, tiled=True)  23 us
    all_to_all x1, waiting for transfers between devices, per_device(): parts = lax.all_to_all(parts, ('band', 'z_lo'), 0, 0, tiled=True)  15.4 us
    pallas_call x1, Pallas kernels, per_device(): pl.pallas_call(gram_kernel, in_specs=[smem, hbm, hbm, hbm, hbm], out_spec...  3.83 us
    pallas_call x1, Pallas kernels, per_device(): pl.pallas_call(block_kernel, in_specs=[smem, smem, vmem, vmem], out_specs...  1.69 us
  transfers between devices with their start and end apart: 1, of which 1 were waited for; matrix products, arithmetic and copies ran while one was open for 0% of the time, Pallas kernels for 0%

profile of v3, /device:TPU:1, one launch (start us, length us, event | category | flops | bytes accessed | tf_op | source)
XLA Modules:
  0.0 70.8 jit_solution(4598168497776273170)
XLA Ops:
  0.6 3.8 %gram.1 = (bf16[32,4,8,256]{3,2,1,0:T(8,128)(2,1)S(1)}, bf16[6,2,128,128]{3,2,1,0:T(8,128)(2,1)S(1)}) custom-call(s32[1]{0:T(128)} %bitcast.1.base_ref, s32[1,3]{1,0:T(1,128)} %mom_hbm.1, s32[1,6]{1,0:T(1,128)} %pairs_hbm.1, bf16[8,2,3,168,128]{4,3,2,1,0:T(8,128)(2,1)} %evecs_hbm.1, bf16[32,2,128,128]{3,2,1,0:T(8,128)(2,1)} %bitcast.8), custom_call_target="tpu_custom_call" | custom-call | tf_op jit(solution)/shard_map/gram/pallas_call | solution.py:127
  4.5 23.0 %all_to_all.10.parts_ref = bf16[32,4,8,256]{3,2,1,0:T(8,128)(2,1)S(1)} all-to-all(bf16[32,4,8,256]{3,2,1,0:T(8,128)(2,1)S(1)} %get-tuple-element.6), channel_id=1, replica_groups=mesh['tm'=8,'band'=8,'z_lo'=4,'x'=4] {'tm','x'}, dimensions={0} | all-to-all | bytes 1048576 | tf_op jit(solution)/shard_map/all_to_all | solution.py:147
  27.4 0.7 %total.1 = bf16[8,4,8,256]{3,2,1,0:T(8,128)(2,1)} custom-call(bf16[32,4,8,256]{3,2,1,0:T(8,128)(2,1)S(1)} %all_to_all.10.parts_ref), custom_call_target="tpu_custom_call" | custom-call | tf_op jit(solution)/shard_map/total/pallas_call | solution.py:148
  28.2 24.9 %all-to-all-start.1 = ((bf16[32,8,256]{2,1,0:T(8,128)(2,1)}), bf16[32,8,256]{2,1,0:T(8,128)(2,1)S(1)}, u32[]{:S(2)}, u32[]{:S(2)}) async-start(bf16[32,8,256]{2,1,0:T(8,128)(2,1)} %bitcast.3), calls=%async_computation.1 | async-start | bytes 262144 | tf_op jit(solution)/shard_map/all_to_all | solution.py:157
  53.8 15.4 %all-to-all-done.1 = bf16[32,8,256]{2,1,0:T(8,128)(2,1)S(1)} async-done(((bf16[32,8,256]{2,1,0:T(8,128)(2,1)}), bf16[32,8,256]{2,1,0:T(8,128)(2,1)S(1)}, u32[]{:S(2)}, u32[]{:S(2)}) %all-to-all-start.1) | async-done | bytes 131104 | tf_op jit(solution)/shard_map/all_to_all | solution.py:157
  69.1 1.7 %blocks.1 = (f32[8,1,256]{2,1,0:T(1,128)}, f32[6,8,8,256]{3,2,1,0:T(8,128)}) custom-call(s32[1]{0:T(128)} %bitcast.band_ref, s32[1]{0:T(128)S(6)} %copy.7.counts_ref, bf16[8,4,8,256]{3,2,1,0:T(8,128)(2,1)S(1)} %bitcast.7, bf16[6,2,128,128]{3,2,1,0:T(8,128)(2,1)S(1)} %get-tuple-element.7.chosen_ref), custom_call_target="tpu_custom_call" | custom-call | tf_op jit(solution)/shard_map/blocks/pallas_call | solution.py:158
Async XLA Ops:
  28.2 40.9 %all-to-all-start.1 = ((bf16[32,8,256]{2,1,0:T(8,128)(2,1)}), bf16[32,8,256]{2,1,0:T(8,128)(2,1)S(1)}, u32[]{:S(2)}, u32[]{:S(2)}) async-start(bf16[32,8,256]{2,1,0:T(8,128)(2,1)} %bitcast.3), calls=%async_computation.1 | async-start | bytes 262144 | tf_op jit(solution)/shard_map/all_to_all | solution.py:157

commit v4 on v3

--- a/solution.py
+++ b/solution.py
@@ -44,30 +44,40 @@
     theta = wave.astype(jnp.float32) * jnp.float32(2.0 * math.pi / EXTENT)
     cosine = jnp.cos(theta)
     sine = jnp.sin(theta)
-    for t in range(tcount):
-        loads[t].wait()
-        slot = t % 2
+
+    def rotate(t):
         for colour in range(colours):
-            real = evecs_ref[t, 0, colour]
-            imag = evecs_ref[t, 1, colour]
-            vreal = real.astype(jnp.float32)
-            vimag = imag.astype(jnp.float32)
-            right_ref[slot, colour, :, :nvec] = (cosine * vreal + sine * vimag).astype(jnp.bfloat16)
-            right_ref[slot, colour, :, nvec:] = (cosine * vimag - sine * vreal).astype(jnp.bfloat16)
-        acc = jnp.concatenate([lax.dot_general(
-            evecs_ref[t, q].reshape(colours * sites, nvec),
-            right_ref[slot].reshape(colours * sites, 2 * nvec),
-            (((0,), (0,)), ((), ())),
-            preferred_element_type=jnp.float32,
-        ) for q in range(2)], axis=0)
+            vreal = evecs_ref[t, 0, colour].astype(jnp.float32)
+            vimag = evecs_ref[t, 1, colour].astype(jnp.float32)
+            right_ref[t, colour, :, :nvec] = (cosine * vreal + sine * vimag).astype(jnp.bfloat16)
+            right_ref[t, colour, :, nvec:] = (cosine * vimag - sine * vreal).astype(jnp.bfloat16)
+
+    def multiply(t):
+        right = right_ref[t].reshape(colours * sites, 2 * nvec)
+        with_real, with_imag = (
+            lax.dot_general(
+                evecs_ref[t, part].reshape(colours * sites, nvec),
+                right,
+                (((0,), (0,)), ((), ())),
+                preferred_element_type=jnp.float32,
+            )
+            for part in range(2)
+        )
         meson = jnp.concatenate(
-            [acc[:nvec, :nvec] + acc[nvec:, nvec:], acc[:nvec, nvec:] - acc[nvec:, :nvec]], axis=1
-        )
-        meson = meson.astype(out_ref.dtype)
+            [with_real[:, :nvec] + with_imag[:, nvec:], with_real[:, nvec:] - with_imag[:, :nvec]], axis=1
+        ).astype(out_ref.dtype)
         for x in range(n_x):
             for zl in range(n_zl):
                 first = (zl * n_x + x) * rows
                 out_ref[t * n_x + x, zl] = meson[first : first + rows]
+
+    groups = [list(range(4)), list(range(4, 8))]
+    for g, group in enumerate(groups):
+        for t in group:
+            loads[t].wait()
+        for t in group:
+            rotate(t)
+            multiply(t)
     for copy in picks:
         copy.wait()
 
@@ -78,34 +88,34 @@
         out_ref[band] = total
 
 
-def block_kernel(band_ref, counts_ref, parts_ref, chosen_ref, meson_ref, out_hbm, total_ref, out_ref, sems):
+def block_kernel(band_ref, counts_ref, parts_ref, chosen_ref, meson_hbm, out_hbm, total_ref, meson_ref, out_ref, sems):
     moms, _, rows, width = parts_ref.shape
     slots = out_ref.shape[0]
     size = moms * rows
     nvec = width // 2
     total_ref[...] = jnp.sum(parts_ref[...].astype(jnp.float32), axis=1)
-    left = total_ref[...].astype(jnp.bfloat16).reshape(size, width)
-    to = lax.broadcasted_iota(jnp.int32, (size, size), 0)
-    frm = lax.broadcasted_iota(jnp.int32, (size, size), 1)
-    swap = jnp.where((to // moms == frm % rows) & (to % moms == frm // rows), 1.0, 0.0).astype(jnp.bfloat16)
-    left = jnp.dot(swap, left, preferred_element_type=jnp.float32)
+    own = total_ref[band_ref[0]]
+    for row in range(rows):
+        meson_ref[row] = own[row : row + 1]
+    meson_copy = pltpu.make_async_copy(meson_ref, meson_hbm, sems.at[slots])
+    meson_copy.start()
+    left = jnp.swapaxes(total_ref[...], 0, 1).reshape(size, width)
     mreal = left[:, :nvec]
     mimag = left[:, nvec:]
     both = jnp.concatenate(
         [jnp.concatenate([mreal, -mimag], axis=1), jnp.concatenate([mimag, mreal], axis=1)], axis=0
     ).astype(jnp.bfloat16)
-    copies = []
-    for c in range(slots):
-        right = chosen_ref[c].reshape(width, nvec)
-        prod = jnp.dot(both, right, preferred_element_type=jnp.float32)
-        prod = jnp.where(c < counts_ref[0], prod, 0.0)
-        out_ref[c, :, :, :nvec] = prod[:size].reshape(rows, moms, nvec)
-        out_ref[c, :, :, nvec:] = prod[size:].reshape(rows, moms, nvec)
-        copies.append(pltpu.make_async_copy(out_ref.at[c], out_hbm.at[c], sems.at[c]))
-        copies[-1].start()
-    own = total_ref[band_ref[0]]
-    for row in range(rows):
-        meson_ref[row] = own[row : row + 1]
+    copies = [meson_copy]
+    for pair in range(slots // 2):
+        right = jnp.concatenate([chosen_ref[2 * pair + q].reshape(width, nvec) for q in range(2)], axis=1)
+        prods = jnp.dot(both, right, preferred_element_type=jnp.float32)
+        for q in range(2):
+            c = 2 * pair + q
+            prod = jnp.where(c < counts_ref[0], prods[:, q * nvec : (q + 1) * nvec], 0.0)
+            out_ref[c, :, :, :nvec] = prod[:size].reshape(rows, moms, nvec)
+            out_ref[c, :, :, nvec:] = prod[size:].reshape(rows, moms, nvec)
+            copies.append(pltpu.make_async_copy(out_ref.at[c], out_hbm.at[c], sems.at[c]))
+            copies[-1].start()
     for copy in copies:
         copy.wait()
 
@@ -134,7 +144,7 @@
         ],
         scratch_shapes=[
             pltpu.VMEM((tcount, 2, colours, piece_len, nvec), jnp.bfloat16),
-            pltpu.VMEM((2, colours, piece_len, width), jnp.bfloat16),
+            pltpu.VMEM((tcount, colours, piece_len, width), jnp.bfloat16),
             pltpu.SMEM(mom.shape, jnp.int32),
             pltpu.SMEM(pairs.shape, jnp.int32),
             pltpu.SemaphoreType.DMA((tcount,)),
@@ -158,15 +168,16 @@
     meson, blocks = pl.pallas_call(
         block_kernel,
         in_specs=[smem, smem, vmem, vmem],
-        out_specs=[vmem, hbm],
+        out_specs=[hbm, hbm],
         out_shape=[
             jax.ShapeDtypeStruct((rows, 1, width), jnp.float32),
             jax.ShapeDtypeStruct((slots, rows, n_band, width), jnp.float32),
         ],
         scratch_shapes=[
             pltpu.VMEM((n_band, rows, width), jnp.float32),
+            pltpu.VMEM((rows, 1, width), jnp.float32),
             pltpu.VMEM((slots, rows, n_band, width), jnp.float32),
-            pltpu.SemaphoreType.DMA((slots,)),
+            pltpu.SemaphoreType.DMA((slots + 1,)),
         ],
         compiler_params=pltpu.CompilerParams(vmem_limit_bytes=8 << 20),
         name="blocks",

time: 71.1 us -> 69.5 us (0.977)
  Pallas kernels: 6.25 us -> 4.65 us
    pallas_call x1, Pallas kernels: 3.83 us -> 2.91 us  [per_device(): pl.pallas_call(gram_kernel, in_specs=[smem, hbm, hbm, hbm, hbm], out_spec...]
where the time goes in v4:
time: 69.5 us; the launch traced here: 69.2 us
  starting transfers between devices  24.9 us (36%)
  blocking collectives  23 us (33%)
  waiting for transfers between devices  15.4 us (22%)
  Pallas kernels  4.65 us (7%)
  between operations  1.31 us (2%)
    all_to_all x1, starting transfers between devices, per_device(): parts = lax.all_to_all(parts, ('band', 'z_lo'), 0, 0, tiled=True)  24.9 us
    all_to_all x1, blocking collectives, per_device(): parts = lax.all_to_all(parts, ('tm', 'x'), 0, 0, tiled=True)  23 us
    all_to_all x1, waiting for transfers between devices, per_device(): parts = lax.all_to_all(parts, ('band', 'z_lo'), 0, 0, tiled=True)  15.4 us
    pallas_call x1, Pallas kernels, per_device(): pl.pallas_call(gram_kernel, in_specs=[smem, hbm, hbm, hbm, hbm], out_spec...  2.91 us
  transfers between devices with their start and end apart: 1, of which 1 were waited for; matrix products, arithmetic and copies ran while one was open for 0% of the time, Pallas kernels for 0%

profile of v4, /device:TPU:1, one launch (start us, length us, event | category | flops | bytes accessed | tf_op | source)
XLA Modules:
  0.0 69.2 jit_solution(17720867549376346293)
XLA Ops:
  0.6 2.9 %gram.1 = (bf16[32,4,8,256]{3,2,1,0:T(8,128)(2,1)S(1)}, bf16[6,2,128,128]{3,2,1,0:T(8,128)(2,1)S(1)}) custom-call(s32[1]{0:T(128)} %bitcast.1.base_ref, s32[1,3]{1,0:T(1,128)} %mom_hbm.1, s32[1,6]{1,0:T(1,128)} %pairs_hbm.1, bf16[8,2,3,168,128]{4,3,2,1,0:T(8,128)(2,1)} %evecs_hbm.1, bf16[32,2,128,128]{3,2,1,0:T(8,128)(2,1)} %bitcast.8), custom_call_target="tpu_custom_call" | custom-call | tf_op jit(solution)/shard_map/gram/pallas_call | solution.py:137
  3.6 23.0 %all_to_all.10.parts_ref = bf16[32,4,8,256]{3,2,1,0:T(8,128)(2,1)S(1)} all-to-all(bf16[32,4,8,256]{3,2,1,0:T(8,128)(2,1)S(1)} %get-tuple-element.6), channel_id=1, replica_groups=mesh['tm'=8,'band'=8,'z_lo'=4,'x'=4] {'tm','x'}, dimensions={0} | all-to-all | bytes 1048576 | tf_op jit(solution)/shard_map/all_to_all | solution.py:157
  26.5 0.7 %total.1 = bf16[8,4,8,256]{3,2,1,0:T(8,128)(2,1)} custom-call(bf16[32,4,8,256]{3,2,1,0:T(8,128)(2,1)S(1)} %all_to_all.10.parts_ref), custom_call_target="tpu_custom_call" | custom-call | tf_op jit(solution)/shard_map/total/pallas_call | solution.py:158
  27.3 24.9 %all-to-all-start.1 = ((bf16[32,8,256]{2,1,0:T(8,128)(2,1)}), bf16[32,8,256]{2,1,0:T(8,128)(2,1)S(1)}, u32[]{:S(2)}, u32[]{:S(2)}) async-start(bf16[32,8,256]{2,1,0:T(8,128)(2,1)} %bitcast.3), calls=%async_computation.1 | async-start | bytes 262144 | tf_op jit(solution)/shard_map/all_to_all | solution.py:167
  52.8 15.4 %all-to-all-done.1 = bf16[32,8,256]{2,1,0:T(8,128)(2,1)S(1)} async-done(((bf16[32,8,256]{2,1,0:T(8,128)(2,1)}), bf16[32,8,256]{2,1,0:T(8,128)(2,1)S(1)}, u32[]{:S(2)}, u32[]{:S(2)}) %all-to-all-start.1) | async-done | bytes 131104 | tf_op jit(solution)/shard_map/all_to_all | solution.py:167
  68.2 1.0 %blocks.1 = (f32[8,1,256]{2,1,0:T(1,128)}, f32[6,8,8,256]{3,2,1,0:T(8,128)}) custom-call(s32[1]{0:T(128)} %bitcast.band_ref, s32[1]{0:T(128)S(6)} %copy.7.counts_ref, bf16[8,4,8,256]{3,2,1,0:T(8,128)(2,1)S(1)} %bitcast.7, bf16[6,2,128,128]{3,2,1,0:T(8,128)(2,1)S(1)} %get-tuple-element.7.chosen_ref), custom_call_target="tpu_custom_call" | custom-call | tf_op jit(solution)/shard_map/blocks/pallas_call | solution.py:168
Async XLA Ops:
  27.3 40.9 %all-to-all-start.1 = ((bf16[32,8,256]{2,1,0:T(8,128)(2,1)}), bf16[32,8,256]{2,1,0:T(8,128)(2,1)S(1)}, u32[]{:S(2)}, u32[]{:S(2)}) async-start(bf16[32,8,256]{2,1,0:T(8,128)(2,1)} %bitcast.3), calls=%async_computation.1 | async-start | bytes 262144 | tf_op jit(solution)/shard_map/all_to_all | solution.py:167

commit v5 on v4

--- a/solution.py
+++ b/solution.py
@@ -9,6 +9,7 @@
 
 EXTENT = 64
 Z_LO = 4
+CORES = 2
 
 
 def gram_kernel(
@@ -69,7 +70,7 @@
         for x in range(n_x):
             for zl in range(n_zl):
                 first = (zl * n_x + x) * rows
-                out_ref[t * n_x + x, zl] = meson[first : first + rows]
+                out_ref[x * tcount + t, zl] = meson[first : first + rows]
 
     groups = [list(range(4)), list(range(4, 8))]
     for g, group in enumerate(groups):
@@ -89,11 +90,14 @@
 
 
 def block_kernel(band_ref, counts_ref, parts_ref, chosen_ref, meson_hbm, out_hbm, total_ref, meson_ref, out_ref, sems):
-    moms, _, rows, width = parts_ref.shape
+    cores, n_zh, _, rows, width = parts_ref.shape
+    moms = cores * n_zh
     slots = out_ref.shape[0]
     size = moms * rows
     nvec = width // 2
-    total_ref[...] = jnp.sum(parts_ref[...].astype(jnp.float32), axis=1)
+    for core in range(cores):
+        for zh in range(n_zh):
+            total_ref[zh * cores + core] = jnp.sum(parts_ref[core, zh].astype(jnp.float32), axis=0)
     own = total_ref[band_ref[0]]
     for row in range(rows):
         meson_ref[row] = own[row : row + 1]
@@ -125,7 +129,9 @@
     n_tm = lax.axis_size("tm")
     n_zl = lax.axis_size("z_lo")
     n_x = lax.axis_size("x")
-    n_band = lax.axis_size("band")
+    n_zh = lax.axis_size("z_hi")
+    n_core = lax.axis_size("core")
+    n_band = n_zh * n_core
     slots = pairs.shape[1]
     rows = nvec // (n_zl * n_x)
     width = 2 * nvec
@@ -154,7 +160,7 @@
         compiler_params=pltpu.CompilerParams(vmem_limit_bytes=16 << 20),
         name="gram",
     )(base.reshape(1), *(pltpu.with_memory_space_constraint(a, pltpu.HBM) for a in (mom, pairs, evecs, peram[0])))
-    parts = lax.all_to_all(parts, ("tm", "x"), 0, 0, tiled=True)
+    parts = lax.all_to_all(parts, ("x", "tm"), 0, 0, tiled=True)
     parts = pl.pallas_call(
         sum_kernel,
         in_specs=[vmem],
@@ -164,7 +170,7 @@
         name="total",
     )(parts)
     parts = parts.reshape(n_band * n_zl, rows, width)
-    parts = lax.all_to_all(parts, ("band", "z_lo"), 0, 0, tiled=True)
+    parts = lax.all_to_all(parts, ("core", "z_hi", "z_lo"), 0, 0, tiled=True)
     meson, blocks = pl.pallas_call(
         block_kernel,
         in_specs=[smem, smem, vmem, vmem],
@@ -182,9 +188,9 @@
         compiler_params=pltpu.CompilerParams(vmem_limit_bytes=8 << 20),
         name="blocks",
     )(
-        lax.axis_index("band").astype(jnp.int32).reshape(1),
+        (lax.axis_index("z_hi") * n_core + lax.axis_index("core")).astype(jnp.int32).reshape(1),
         counts,
-        parts.reshape(n_band, n_zl, rows, width),
+        parts.reshape(n_core, n_zh, n_zl, rows, width),
         chosen,
     )
     return meson[None], blocks[None]
@@ -192,17 +198,21 @@
 
 def solution(mesh):
     n_tm, n_band, n_space = (mesh.shape[name] for name in ("tm", "band", "space"))
-    fine = Mesh(mesh.devices.reshape(n_tm, n_band, Z_LO, n_space // Z_LO), ("tm", "band", "z_lo", "x"))
+    fine = Mesh(
+        mesh.devices.reshape(n_tm, n_band // CORES, CORES, Z_LO, n_space // Z_LO),
+        ("tm", "z_hi", "core", "z_lo", "x"),
+    )
+    band = ("z_hi", "core")
     return jax.shard_map(
         per_device,
         mesh=fine,
         in_specs=(
             P(None, None, None, ("tm", "z_lo", "x"), None),
             P("tm", None, None, None, None),
-            P("band", None),
-            P("band", None),
-            P("band"),
+            P(band, None),
+            P(band, None),
+            P(band),
         ),
-        out_specs=(P("tm", ("z_lo", "x"), "band", None), P("tm", "band", ("z_lo", "x"), None, None)),
+        out_specs=(P("tm", ("z_lo", "x"), band, None), P("tm", band, ("z_lo", "x"), None, None)),
         check_vma=False,
     )

time: 69.5 us -> 69.1 us (level)
  blocking collectives: 23 us -> 21.7 us
    all_to_all x1, blocking collectives: 23 us -> 21.7 us  [per_device(): parts = lax.all_to_all(parts, ('x', 'tm'), 0, 0, tiled=True)]
where the time goes in v5:
time: 69.1 us; the launch traced here: 68.7 us
  starting transfers between devices  25.3 us (37%)
  blocking collectives  21.7 us (31%)
  waiting for transfers between devices  15.7 us (23%)
  Pallas kernels  4.65 us (7%)
  between operations  1.31 us (2%)
    all_to_all x1, starting transfers between devices, per_device(): parts = lax.all_to_all(parts, ('core', 'z_hi', 'z_lo'), 0, 0, tiled=True)  25.3 us
    all_to_all x1, blocking collectives, per_device(): parts = lax.all_to_all(parts, ('x', 'tm'), 0, 0, tiled=True)  21.7 us
    all_to_all x1, waiting for transfers between devices, per_device(): parts = lax.all_to_all(parts, ('core', 'z_hi', 'z_lo'), 0, 0, tiled=True)  15.7 us
    pallas_call x1, Pallas kernels, per_device(): pl.pallas_call(gram_kernel, in_specs=[smem, hbm, hbm, hbm, hbm], out_spec...  2.91 us
  transfers between devices with their start and end apart: 1, of which 1 were waited for; matrix products, arithmetic and copies ran while one was open for 0% of the time, Pallas kernels for 0%

profile of v5, /device:TPU:1, one launch (start us, length us, event | category | flops | bytes accessed | tf_op | source)
XLA Modules:
  0.0 68.7 jit_solution(2803439036113559654)
XLA Ops:
  0.6 2.9 %gram.1 = (bf16[32,4,8,256]{3,2,1,0:T(8,128)(2,1)S(1)}, bf16[6,2,128,128]{3,2,1,0:T(8,128)(2,1)S(1)}) custom-call(s32[1]{0:T(128)} %bitcast.1.base_ref, s32[1,3]{1,0:T(1,128)} %mom_hbm.1, s32[1,6]{1,0:T(1,128)} %pairs_hbm.1, bf16[8,2,3,168,128]{4,3,2,1,0:T(8,128)(2,1)} %evecs_hbm.1, bf16[32,2,128,128]{3,2,1,0:T(8,128)(2,1)} %bitcast.8), custom_call_target="tpu_custom_call" | custom-call | tf_op jit(solution)/shard_map/gram/pallas_call | solution.py:143
  3.6 21.7 %all_to_all.10.parts_ref = bf16[32,4,8,256]{3,2,1,0:T(8,128)(2,1)S(1)} all-to-all(bf16[32,4,8,256]{3,2,1,0:T(8,128)(2,1)S(1)} %get-tuple-element.6), channel_id=1, replica_groups=mesh['tm'=8,'z_hi'=4,'core'=2,'z_lo'=4,'x'=4] {'x','tm'}, dimensions={0} | all-to-all | bytes 1048576 | tf_op jit(solution)/shard_map/all_to_all | solution.py:163
  25.3 0.7 %total.1 = bf16[8,4,8,256]{3,2,1,0:T(8,128)(2,1)} custom-call(bf16[32,4,8,256]{3,2,1,0:T(8,128)(2,1)S(1)} %all_to_all.10.parts_ref), custom_call_target="tpu_custom_call" | custom-call | tf_op jit(solution)/shard_map/total/pallas_call | solution.py:164
  26.0 25.3 %all-to-all-start.1 = ((bf16[32,8,256]{2,1,0:T(8,128)(2,1)}), bf16[32,8,256]{2,1,0:T(8,128)(2,1)S(1)}, u32[]{:S(2)}, u32[]{:S(2)}) async-start(bf16[32,8,256]{2,1,0:T(8,128)(2,1)} %bitcast.3), calls=%async_computation.1 | async-start | bytes 262144 | tf_op jit(solution)/shard_map/all_to_all | solution.py:173
  52.0 15.7 %all-to-all-done.1 = bf16[32,8,256]{2,1,0:T(8,128)(2,1)S(1)} async-done(((bf16[32,8,256]{2,1,0:T(8,128)(2,1)}), bf16[32,8,256]{2,1,0:T(8,128)(2,1)S(1)}, u32[]{:S(2)}, u32[]{:S(2)}) %all-to-all-start.1) | async-done | bytes 131104 | tf_op jit(solution)/shard_map/all_to_all | solution.py:173
  67.7 1.0 %blocks.1 = (f32[8,1,256]{2,1,0:T(1,128)}, f32[6,8,8,256]{3,2,1,0:T(8,128)}) custom-call(s32[1]{0:T(128)} %bitcast.band_ref, s32[1]{0:T(128)S(6)} %copy.7.counts_ref, bf16[2,4,4,8,256]{4,3,2,1,0:T(8,128)(2,1)S(1)} %bitcast.7, bf16[6,2,128,128]{3,2,1,0:T(8,128)(2,1)S(1)} %get-tuple-element.7.chosen_ref), custom_call_target="tpu_custom_call" | custom-call | tf_op jit(solution)/shard_map/blocks/pallas_call | solution.py:174
Async XLA Ops:
  26.0 41.7 %all-to-all-start.1 = ((bf16[32,8,256]{2,1,0:T(8,128)(2,1)}), bf16[32,8,256]{2,1,0:T(8,128)(2,1)S(1)}, u32[]{:S(2)}, u32[]{:S(2)}) async-start(bf16[32,8,256]{2,1,0:T(8,128)(2,1)} %bitcast.3), calls=%async_computation.1 | async-start | bytes 262144 | tf_op jit(solution)/shard_map/all_to_all | solution.py:173

commit v6 on v5

--- a/solution.py
+++ b/solution.py
@@ -85,19 +85,20 @@
 
 def sum_kernel(parts_ref, out_ref):
     total = jnp.sum(parts_ref[...].astype(jnp.float32), axis=0).astype(jnp.bfloat16)
-    for band in range(out_ref.shape[0]):
-        out_ref[band] = total
+    for zh in range(out_ref.shape[0]):
+        for core in range(out_ref.shape[2]):
+            out_ref[zh, :, core] = total
 
 
 def block_kernel(band_ref, counts_ref, parts_ref, chosen_ref, meson_hbm, out_hbm, total_ref, meson_ref, out_ref, sems):
-    cores, n_zh, _, rows, width = parts_ref.shape
+    n_zh, _, cores, rows, width = parts_ref.shape
     moms = cores * n_zh
     slots = out_ref.shape[0]
     size = moms * rows
     nvec = width // 2
     for core in range(cores):
         for zh in range(n_zh):
-            total_ref[zh * cores + core] = jnp.sum(parts_ref[core, zh].astype(jnp.float32), axis=0)
+            total_ref[zh * cores + core] = jnp.sum(parts_ref[zh, :, core].astype(jnp.float32), axis=0)
     own = total_ref[band_ref[0]]
     for row in range(rows):
         meson_ref[row] = own[row : row + 1]
@@ -165,12 +166,12 @@
         sum_kernel,
         in_specs=[vmem],
         out_specs=vmem,
-        out_shape=jax.ShapeDtypeStruct((n_band, n_zl, rows, width), jnp.bfloat16),
+        out_shape=jax.ShapeDtypeStruct((n_zh, n_zl, n_core, rows, width), jnp.bfloat16),
         compiler_params=pltpu.CompilerParams(vmem_limit_bytes=8 << 20),
         name="total",
     )(parts)
     parts = parts.reshape(n_band * n_zl, rows, width)
-    parts = lax.all_to_all(parts, ("core", "z_hi", "z_lo"), 0, 0, tiled=True)
+    parts = lax.all_to_all(parts, ("z_hi", "z_lo", "core"), 0, 0, tiled=True)
     meson, blocks = pl.pallas_call(
         block_kernel,
         in_specs=[smem, smem, vmem, vmem],
@@ -190,7 +191,7 @@
     )(
         (lax.axis_index("z_hi") * n_core + lax.axis_index("core")).astype(jnp.int32).reshape(1),
         counts,
-        parts.reshape(n_core, n_zh, n_zl, rows, width),
+        parts.reshape(n_zh, n_zl, n_core, rows, width),
         chosen,
     )
     return meson[None], blocks[None]

time: 69.1 us -> 69.5 us (level); the launches traced: 68.7 us -> 68.2 us
  no operation moved by 1% of the time
where the time goes in v6:
time: 69.5 us; the launch traced here: 68.2 us
  starting transfers between devices  25.3 us (36%)
  blocking collectives  21.7 us (31%)
  waiting for transfers between devices  15.2 us (22%)
  Pallas kernels  4.65 us (7%)
  between operations  1.31 us (2%)
    all_to_all x1, starting transfers between devices, per_device(): parts = lax.all_to_all(parts, ('z_hi', 'z_lo', 'core'), 0, 0, tiled=True)  25.3 us
    all_to_all x1, blocking collectives, per_device(): parts = lax.all_to_all(parts, ('x', 'tm'), 0, 0, tiled=True)  21.7 us
    all_to_all x1, waiting for transfers between devices, per_device(): parts = lax.all_to_all(parts, ('z_hi', 'z_lo', 'core'), 0, 0, tiled=True)  15.2 us
    pallas_call x1, Pallas kernels, per_device(): pl.pallas_call(gram_kernel, in_specs=[smem, hbm, hbm, hbm, hbm], out_spec...  2.91 us
  transfers between devices with their start and end apart: 1, of which 1 were waited for; matrix products, arithmetic and copies ran while one was open for 0% of the time, Pallas kernels for 0%

profile of v6, /device:TPU:1, one launch (start us, length us, event | category | flops | bytes accessed | tf_op | source)
XLA Modules:
  0.0 68.2 jit_solution(4386878639262347980)
XLA Ops:
  0.6 2.9 %gram.1 = (bf16[32,4,8,256]{3,2,1,0:T(8,128)(2,1)S(1)}, bf16[6,2,128,128]{3,2,1,0:T(8,128)(2,1)S(1)}) custom-call(s32[1]{0:T(128)} %bitcast.1.base_ref, s32[1,3]{1,0:T(1,128)} %mom_hbm.1, s32[1,6]{1,0:T(1,128)} %pairs_hbm.1, bf16[8,2,3,168,128]{4,3,2,1,0:T(8,128)(2,1)} %evecs_hbm.1, bf16[32,2,128,128]{3,2,1,0:T(8,128)(2,1)} %bitcast.8), custom_call_target="tpu_custom_call" | custom-call | tf_op jit(solution)/shard_map/gram/pallas_call | solution.py:144
  3.6 21.7 %all_to_all.10.parts_ref = bf16[32,4,8,256]{3,2,1,0:T(8,128)(2,1)S(1)} all-to-all(bf16[32,4,8,256]{3,2,1,0:T(8,128)(2,1)S(1)} %get-tuple-element.6), channel_id=1, replica_groups=mesh['tm'=8,'z_hi'=4,'core'=2,'z_lo'=4,'x'=4] {'x','tm'}, dimensions={0} | all-to-all | bytes 1048576 | tf_op jit(solution)/shard_map/all_to_all | solution.py:164
  25.3 0.7 %total.1 = bf16[4,4,2,8,256]{4,3,2,1,0:T(8,128)(2,1)} custom-call(bf16[32,4,8,256]{3,2,1,0:T(8,128)(2,1)S(1)} %all_to_all.10.parts_ref), custom_call_target="tpu_custom_call" | custom-call | tf_op jit(solution)/shard_map/total/pallas_call | solution.py:165
  26.0 25.3 %all-to-all-start.1 = ((bf16[32,8,256]{2,1,0:T(8,128)(2,1)}), bf16[32,8,256]{2,1,0:T(8,128)(2,1)S(1)}, u32[]{:S(2)}, u32[]{:S(2)}) async-start(bf16[32,8,256]{2,1,0:T(8,128)(2,1)} %bitcast.3), calls=%async_computation.1 | async-start | bytes 262144 | tf_op jit(solution)/shard_map/all_to_all | solution.py:174
  52.0 15.2 %all-to-all-done.1 = bf16[32,8,256]{2,1,0:T(8,128)(2,1)S(1)} async-done(((bf16[32,8,256]{2,1,0:T(8,128)(2,1)}), bf16[32,8,256]{2,1,0:T(8,128)(2,1)S(1)}, u32[]{:S(2)}, u32[]{:S(2)}) %all-to-all-start.1) | async-done | bytes 131104 | tf_op jit(solution)/shard_map/all_to_all | solution.py:174
  67.2 1.0 %blocks.1 = (f32[8,1,256]{2,1,0:T(1,128)}, f32[6,8,8,256]{3,2,1,0:T(8,128)}) custom-call(s32[1]{0:T(128)} %bitcast.band_ref, s32[1]{0:T(128)S(6)} %copy.7.counts_ref, bf16[4,4,2,8,256]{4,3,2,1,0:T(8,128)(2,1)S(1)} %bitcast.7, bf16[6,2,128,128]{3,2,1,0:T(8,128)(2,1)S(1)} %get-tuple-element.7.chosen_ref), custom_call_target="tpu_custom_call" | custom-call | tf_op jit(solution)/shard_map/blocks/pallas_call | solution.py:175
Async XLA Ops:
  26.0 41.2 %all-to-all-start.1 = ((bf16[32,8,256]{2,1,0:T(8,128)(2,1)}), bf16[32,8,256]{2,1,0:T(8,128)(2,1)S(1)}, u32[]{:S(2)}, u32[]{:S(2)}) async-start(bf16[32,8,256]{2,1,0:T(8,128)(2,1)} %bitcast.3), calls=%async_computation.1 | async-start | bytes 262144 | tf_op jit(solution)/shard_map/all_to_all | solution.py:174

commit v7 on v5

--- a/solution.py
+++ b/solution.py
@@ -1,3 +1,4 @@
+import functools
 import math
 
 import jax
@@ -13,34 +14,23 @@
 
 
 def gram_kernel(
-    base_ref, mom_hbm, pairs_hbm, evecs_hbm, peram_hbm, out_ref, chosen_ref,
-    evecs_ref, right_ref, mom_ref, pairs_ref, evecs_sems, small_sems, pick_sems,
+    base_ref, mom_hbm, evecs_hbm, out_ref, evecs_ref, right_ref, mom_ref, evecs_sems, mom_sem
 ):
     tcount, _, colours, sites, nvec = evecs_ref.shape
-    slots = chosen_ref.shape[0]
     n_x = out_ref.shape[0] // tcount
     n_zl, rows = out_ref.shape[1:3]
-    small = [
-        pltpu.make_async_copy(mom_hbm, mom_ref, small_sems.at[0]),
-        pltpu.make_async_copy(pairs_hbm, pairs_ref, small_sems.at[1]),
-    ]
+    mom_copy = pltpu.make_async_copy(mom_hbm, mom_ref, mom_sem)
+    mom_copy.start()
     loads = [
         pltpu.make_async_copy(evecs_hbm.at[t], evecs_ref.at[t], evecs_sems.at[t]) for t in range(tcount)
     ]
-    for copy in small + loads:
+    for copy in loads:
         copy.start()
     site = base_ref[0] + lax.broadcasted_iota(jnp.int32, (sites, nvec), 0)
     xs = site & (EXTENT - 1)
     ys = (site >> 6) & (EXTENT - 1)
     zs = site >> 12
-    for copy in small:
-        copy.wait()
-    picks = [
-        pltpu.make_async_copy(peram_hbm.at[pairs_ref[0, c]], chosen_ref.at[c], pick_sems.at[c])
-        for c in range(slots)
-    ]
-    for copy in picks:
-        copy.start()
+    mom_copy.wait()
     wave = (mom_ref[0, 0] * xs + mom_ref[0, 1] * ys + mom_ref[0, 2] * zs) & (EXTENT - 1)
     theta = wave.astype(jnp.float32) * jnp.float32(2.0 * math.pi / EXTENT)
     cosine = jnp.cos(theta)
@@ -79,25 +69,49 @@
         for t in group:
             rotate(t)
             multiply(t)
-    for copy in picks:
+
+
+def sum_kernel(parts_ref, out_hbm, total_ref, sems):
+    total_ref[...] = jnp.sum(parts_ref[...].astype(jnp.float32), axis=0).astype(jnp.bfloat16)
+    copies = [
+        pltpu.make_async_copy(total_ref, out_hbm.at[band], sems.at[band]) for band in range(out_hbm.shape[0])
+    ]
+    for copy in copies:
+        copy.start()
+    for copy in copies:
         copy.wait()
 
 
-def sum_kernel(parts_ref, out_ref):
-    total = jnp.sum(parts_ref[...].astype(jnp.float32), axis=0).astype(jnp.bfloat16)
-    for band in range(out_ref.shape[0]):
-        out_ref[band] = total
-
-
-def block_kernel(band_ref, counts_ref, parts_ref, chosen_ref, meson_hbm, out_hbm, total_ref, meson_ref, out_ref, sems):
-    cores, n_zh, _, rows, width = parts_ref.shape
+def pick_kernel(counts_ref, pairs_hbm, peram_hbm, out_ref, pairs_ref, pairs_sem, sems):
+    nvec = peram_hbm.shape[-1]
+    pairs_copy = pltpu.make_async_copy(pairs_hbm, pairs_ref, pairs_sem)
+    pairs_copy.start()
+    pairs_copy.wait()
+    copies = [
+        pltpu.make_async_copy(
+            peram_hbm.at[pairs_ref[0, c]], out_ref.at[c // 2, :, :, pl.ds(c % 2 * nvec, nvec)], sems.at[c]
+        )
+        for c in range(pairs_ref.shape[1])
+    ]
+    for copy in copies:
+        copy.start()
+    for c, copy in enumerate(copies):
+        copy.wait()
+
+        @pl.when(c >= counts_ref[0])
+        def _():
+            out_ref[c // 2, :, :, c % 2 * nvec : (c % 2 + 1) * nvec] = jnp.zeros((2, nvec, nvec), out_ref.dtype)
+
+
+def block_kernel(band_ref, parts_ref, chosen_ref, meson_hbm, out_hbm, total_ref, meson_ref, out_ref, sems):
+    n_zh, cores, _, rows, width = parts_ref.shape
     moms = cores * n_zh
     slots = out_ref.shape[0]
     size = moms * rows
     nvec = width // 2
     for core in range(cores):
         for zh in range(n_zh):
-            total_ref[zh * cores + core] = jnp.sum(parts_ref[core, zh].astype(jnp.float32), axis=0)
+            total_ref[zh * cores + core] = jnp.sum(parts_ref[zh, core].astype(jnp.float32), axis=0)
     own = total_ref[band_ref[0]]
     for row in range(rows):
         meson_ref[row] = own[row : row + 1]
@@ -111,11 +125,11 @@
     ).astype(jnp.bfloat16)
     copies = [meson_copy]
     for pair in range(slots // 2):
-        right = jnp.concatenate([chosen_ref[2 * pair + q].reshape(width, nvec) for q in range(2)], axis=1)
+        right = chosen_ref[pair].reshape(width, 2 * nvec)
         prods = jnp.dot(both, right, preferred_element_type=jnp.float32)
         for q in range(2):
             c = 2 * pair + q
-            prod = jnp.where(c < counts_ref[0], prods[:, q * nvec : (q + 1) * nvec], 0.0)
+            prod = prods[:, q * nvec : (q + 1) * nvec]
             out_ref[c, :, :, :nvec] = prod[:size].reshape(rows, moms, nvec)
             out_ref[c, :, :, nvec:] = prod[size:].reshape(rows, moms, nvec)
             copies.append(pltpu.make_async_copy(out_ref.at[c], out_hbm.at[c], sems.at[c]))
@@ -137,43 +151,54 @@
     width = 2 * nvec
     place = (lax.axis_index("tm") * n_zl + lax.axis_index("z_lo")) * n_x + lax.axis_index("x")
     base = (place * piece_len).astype(jnp.int32)
+    hold = functools.partial(pltpu.with_memory_space_constraint, memory_space=pltpu.HBM)
     smem = pl.BlockSpec(memory_space=pltpu.SMEM)
     vmem = pl.BlockSpec(memory_space=pltpu.VMEM)
     hbm = pl.BlockSpec(memory_space=pltpu.HBM)
-    parts, chosen = pl.pallas_call(
+    parts = pl.pallas_call(
         gram_kernel,
-        in_specs=[smem, hbm, hbm, hbm, hbm],
-        out_specs=[vmem, vmem],
-        out_shape=[
-            jax.ShapeDtypeStruct((n_tm * n_x, n_zl, rows, width), jnp.bfloat16),
-            jax.ShapeDtypeStruct((slots, 2, nvec, nvec), jnp.bfloat16),
-        ],
+        in_specs=[smem, hbm, hbm],
+        out_specs=vmem,
+        out_shape=jax.ShapeDtypeStruct((n_tm * n_x, n_zl, rows, width), jnp.bfloat16),
         scratch_shapes=[
             pltpu.VMEM((tcount, 2, colours, piece_len, nvec), jnp.bfloat16),
             pltpu.VMEM((tcount, colours, piece_len, width), jnp.bfloat16),
             pltpu.SMEM(mom.shape, jnp.int32),
-            pltpu.SMEM(pairs.shape, jnp.int32),
             pltpu.SemaphoreType.DMA((tcount,)),
-            pltpu.SemaphoreType.DMA((2,)),
-            pltpu.SemaphoreType.DMA((slots,)),
+            pltpu.SemaphoreType.DMA,
         ],
         compiler_params=pltpu.CompilerParams(vmem_limit_bytes=16 << 20),
         name="gram",
-    )(base.reshape(1), *(pltpu.with_memory_space_constraint(a, pltpu.HBM) for a in (mom, pairs, evecs, peram[0])))
+    )(base.reshape(1), hold(mom), hold(evecs))
     parts = lax.all_to_all(parts, ("x", "tm"), 0, 0, tiled=True)
     parts = pl.pallas_call(
         sum_kernel,
         in_specs=[vmem],
-        out_specs=vmem,
+        out_specs=hbm,
         out_shape=jax.ShapeDtypeStruct((n_band, n_zl, rows, width), jnp.bfloat16),
+        scratch_shapes=[pltpu.VMEM((n_zl, rows, width), jnp.bfloat16), pltpu.SemaphoreType.DMA((n_band,))],
         compiler_params=pltpu.CompilerParams(vmem_limit_bytes=8 << 20),
         name="total",
     )(parts)
     parts = parts.reshape(n_band * n_zl, rows, width)
-    parts = lax.all_to_all(parts, ("core", "z_hi", "z_lo"), 0, 0, tiled=True)
+    parts = lax.all_to_all(parts, ("z_hi", "core", "z_lo"), 0, 0, tiled=True)
+    chosen = pl.pallas_call(
+        pick_kernel,
+        in_specs=[smem, hbm, hbm],
+        out_specs=vmem,
+        out_shape=jax.ShapeDtypeStruct((slots // 2, 2, nvec, 2 * nvec), jnp.bfloat16),
+        scratch_shapes=[
+            pltpu.SMEM(pairs.shape, jnp.int32),
+            pltpu.SemaphoreType.DMA,
+            pltpu.SemaphoreType.DMA((slots,)),
+        ],
+        compiler_params=pltpu.CompilerParams(vmem_limit_bytes=8 << 20),
+        cost_estimate=pl.CostEstimate(flops=0, transcendentals=0, bytes_accessed=8 * slots * nvec * nvec),
+        name="pick",
+    )(counts, hold(pairs), hold(peram[0]))
     meson, blocks = pl.pallas_call(
         block_kernel,
-        in_specs=[smem, smem, vmem, vmem],
+        in_specs=[smem, vmem, vmem],
         out_specs=[hbm, hbm],
         out_shape=[
             jax.ShapeDtypeStruct((rows, 1, width), jnp.float32),
@@ -189,8 +214,7 @@
         name="blocks",
     )(
         (lax.axis_index("z_hi") * n_core + lax.axis_index("core")).astype(jnp.int32).reshape(1),
-        counts,
-        parts.reshape(n_core, n_zh, n_zl, rows, width),
+        parts.reshape(n_zh, n_core, n_zl, rows, width),
         chosen,
     )
     return meson[None], blocks[None]

time: 69.1 us -> 69.2 us (level)
  waiting for transfers between devices: 15.7 us -> 13.6 us
  Pallas kernels: 4.65 us -> 6.36 us
    all_to_all x1, waiting for transfers between devices: 15.7 us -> 13.6 us  [per_device(): parts = lax.all_to_all(parts, ('z_hi', 'core', 'z_lo'), 0, 0, tiled=True)]
    pallas_call x3 -> x4, Pallas kernels: 4.65 us -> 6.36 us  [the longest x1 2.84 us: per_device(): pl.pallas_call(gram_kernel, in_specs=[smem, hbm, hbm], out_specs=vmem, ou...]
  transfers between devices with their start and end apart: 1 -> 1, of which waited for: 1 -> 1; matrix products, arithmetic and copies ran while one was open for 0% -> 0% of each run, Pallas kernels for 0% -> 3%
where the time goes in v7:
time: 69.2 us; the launch traced here: 68.4 us
  starting transfers between devices  25.3 us (37%)
  blocking collectives  21.7 us (31%)
  waiting for transfers between devices  13.6 us (20%)
  Pallas kernels  6.36 us (9%)
  between operations  1.33 us (2%)
    all_to_all x1, starting transfers between devices, per_device(): parts = lax.all_to_all(parts, ('z_hi', 'core', 'z_lo'), 0, 0, tiled=True)  25.3 us
    all_to_all x1, blocking collectives, per_device(): parts = lax.all_to_all(parts, ('x', 'tm'), 0, 0, tiled=True)  21.7 us
    all_to_all x1, waiting for transfers between devices, per_device(): parts = lax.all_to_all(parts, ('z_hi', 'core', 'z_lo'), 0, 0, tiled=True)  13.6 us
    pallas_call x1, Pallas kernels, per_device(): pl.pallas_call(gram_kernel, in_specs=[smem, hbm, hbm], out_specs=vmem, ou...  2.84 us
    pallas_call x1, Pallas kernels, per_device(): pl.pallas_call(pick_kernel, in_specs=[smem, hbm, hbm], out_specs=vmem, ou...  1.74 us
  transfers between devices with their start and end apart: 1, of which 1 were waited for; matrix products, arithmetic and copies ran while one was open for 0% of the time, Pallas kernels for 3%

profile of v7, /device:TPU:1, one launch (start us, length us, event | category | flops | bytes accessed | tf_op | source)
XLA Modules:
  0.0 68.4 jit_solution(7920930676108061590)
XLA Ops:
  0.6 2.8 %gram.1 = bf16[32,4,8,256]{3,2,1,0:T(8,128)(2,1)S(1)} custom-call(s32[1]{0:T(128)} %bitcast.1.base_ref, s32[1,3]{1,0:T(1,128)} %mom_hbm.1, bf16[8,2,3,168,128]{4,3,2,1,0:T(8,128)(2,1)} %evecs_hbm.1), custom_call_target="tpu_custom_call" | custom-call | tf_op jit(solution)/shard_map/gram/pallas_call | solution.py:158
  3.5 21.7 %all_to_all.10.parts_ref = bf16[32,4,8,256]{3,2,1,0:T(8,128)(2,1)S(1)} all-to-all(bf16[32,4,8,256]{3,2,1,0:T(8,128)(2,1)S(1)} %gram.1), channel_id=1, replica_groups=mesh['tm'=8,'z_hi'=4,'core'=2,'z_lo'=4,'x'=4] {'x','tm'}, dimensions={0} | all-to-all | bytes 1048576 | tf_op jit(solution)/shard_map/all_to_all | solution.py:173
  25.2 0.8 %total.1 = bf16[8,4,8,256]{3,2,1,0:T(8,128)(2,1)} custom-call(bf16[32,4,8,256]{3,2,1,0:T(8,128)(2,1)S(1)} %all_to_all.10.parts_ref), custom_call_target="tpu_custom_call" | custom-call | tf_op jit(solution)/shard_map/total/pallas_call | solution.py:174
  26.0 25.3 %all-to-all-start.1 = ((bf16[32,8,256]{2,1,0:T(8,128)(2,1)}), bf16[32,8,256]{2,1,0:T(8,128)(2,1)S(1)}, u32[]{:S(2)}, u32[]{:S(2)}) async-start(bf16[32,8,256]{2,1,0:T(8,128)(2,1)} %bitcast.2), calls=%async_computation.1 | async-start | bytes 262144 | tf_op jit(solution)/shard_map/all_to_all | solution.py:184
  52.0 1.7 %pick.1.chosen_ref = bf16[3,2,128,256]{3,2,1,0:T(8,128)(2,1)S(1)} custom-call(s32[1]{0:T(128)S(6)} %copy.7.counts_ref, s32[1,6]{1,0:T(1,128)} %pairs_hbm.1, bf16[32,2,128,128]{3,2,1,0:T(8,128)(2,1)} %bitcast.8), custom_call_target="tpu_custom_call" | custom-call | bytes 786432 | tf_op jit(solution)/shard_map/pick/pallas_call | solution.py:185
  53.7 13.6 %all-to-all-done.1 = bf16[32,8,256]{2,1,0:T(8,128)(2,1)S(1)} async-done(((bf16[32,8,256]{2,1,0:T(8,128)(2,1)}), bf16[32,8,256]{2,1,0:T(8,128)(2,1)S(1)}, u32[]{:S(2)}, u32[]{:S(2)}) %all-to-all-start.1) | async-done | bytes 131104 | tf_op jit(solution)/shard_map/all_to_all | solution.py:184
  67.4 1.0 %blocks.1 = (f32[8,1,256]{2,1,0:T(1,128)}, f32[6,8,8,256]{3,2,1,0:T(8,128)}) custom-call(s32[1]{0:T(128)} %bitcast.band_ref, bf16[4,2,4,8,256]{4,3,2,1,0:T(8,128)(2,1)S(1)} %bitcast.7, bf16[3,2,128,256]{3,2,1,0:T(8,128)(2,1)S(1)} %pick.1.chosen_ref), custom_call_target="tpu_custom_call" | custom-call | tf_op jit(solution)/shard_map/blocks/pallas_call | solution.py:199
Async XLA Ops:
  26.0 41.4 %all-to-all-start.1 = ((bf16[32,8,256]{2,1,0:T(8,128)(2,1)}), bf16[32,8,256]{2,1,0:T(8,128)(2,1)S(1)}, u32[]{:S(2)}, u32[]{:S(2)}) async-start(bf16[32,8,256]{2,1,0:T(8,128)(2,1)} %bitcast.2), calls=%async_computation.1 | async-start | bytes 262144 | tf_op jit(solution)/shard_map/all_to_all | solution.py:184

commit v8 on v7

--- a/solution.py
+++ b/solution.py
@@ -170,7 +170,9 @@
         compiler_params=pltpu.CompilerParams(vmem_limit_bytes=16 << 20),
         name="gram",
     )(base.reshape(1), hold(mom), hold(evecs))
+    parts = parts.reshape(n_tm * n_x, n_zl * rows, width)
     parts = lax.all_to_all(parts, ("x", "tm"), 0, 0, tiled=True)
+    parts = parts.reshape(n_tm * n_x, n_zl, rows, width)
     parts = pl.pallas_call(
         sum_kernel,
         in_specs=[vmem],

time: 69.2 us -> 69.2 us (level)
  no operation moved by 1% of the time
where the time goes in v8:
time: 69.2 us; the launch traced here: 68.4 us
  starting transfers between devices  25.3 us (37%)
  blocking collectives  21.7 us (31%)
  waiting for transfers between devices  13.6 us (20%)
  Pallas kernels  6.35 us (9%)
  between operations  1.33 us (2%)
    all_to_all x1, starting transfers between devices, per_device(): parts = lax.all_to_all(parts, ('z_hi', 'core', 'z_lo'), 0, 0, tiled=True)  25.3 us
    all_to_all x1, blocking collectives, per_device(): parts = lax.all_to_all(parts, ('x', 'tm'), 0, 0, tiled=True)  21.7 us
    all_to_all x1, waiting for transfers between devices, per_device(): parts = lax.all_to_all(parts, ('z_hi', 'core', 'z_lo'), 0, 0, tiled=True)  13.6 us
    pallas_call x1, Pallas kernels, per_device(): pl.pallas_call(gram_kernel, in_specs=[smem, hbm, hbm], out_specs=vmem, ou...  2.84 us
    pallas_call x1, Pallas kernels, per_device(): pl.pallas_call(pick_kernel, in_specs=[smem, hbm, hbm], out_specs=vmem, ou...  1.73 us
  transfers between devices with their start and end apart: 1, of which 1 were waited for; matrix products, arithmetic and copies ran while one was open for 0% of the time, Pallas kernels for 3%

profile of v8, /device:TPU:1, one launch (start us, length us, event | category | flops | bytes accessed | tf_op | source)
XLA Modules:
  0.0 68.4 jit_solution(7156861568907845617)
XLA Ops:
  0.6 2.8 %gram.1 = bf16[32,4,8,256]{3,2,1,0:T(8,128)(2,1)S(1)} custom-call(s32[1]{0:T(128)} %bitcast.1.base_ref, s32[1,3]{1,0:T(1,128)} %mom_hbm.1, bf16[8,2,3,168,128]{4,3,2,1,0:T(8,128)(2,1)} %evecs_hbm.1), custom_call_target="tpu_custom_call" | custom-call | tf_op jit(solution)/shard_map/gram/pallas_call | solution.py:158
  3.5 21.7 %all_to_all.10 = bf16[32,32,256]{2,1,0:T(8,128)(2,1)S(1)} all-to-all(bf16[32,32,256]{2,1,0:T(8,128)(2,1)S(1)} %bitcast.10), channel_id=1, replica_groups=mesh['tm'=8,'z_hi'=4,'core'=2,'z_lo'=4,'x'=4] {'x','tm'}, dimensions={0} | all-to-all | bytes 1048576 | tf_op jit(solution)/shard_map/all_to_all | solution.py:174
  25.2 0.8 %total.1 = bf16[8,4,8,256]{3,2,1,0:T(8,128)(2,1)} custom-call(bf16[32,4,8,256]{3,2,1,0:T(8,128)(2,1)S(1)} %bitcast.9), custom_call_target="tpu_custom_call" | custom-call | tf_op jit(solution)/shard_map/total/pallas_call | solution.py:176
  26.0 25.3 %all-to-all-start.1 = ((bf16[32,8,256]{2,1,0:T(8,128)(2,1)}), bf16[32,8,256]{2,1,0:T(8,128)(2,1)S(1)}, u32[]{:S(2)}, u32[]{:S(2)}) async-start(bf16[32,8,256]{2,1,0:T(8,128)(2,1)} %bitcast.4), calls=%async_computation.1 | async-start | bytes 262144 | tf_op jit(solution)/shard_map/all_to_all | solution.py:186
  52.0 1.7 %pick.1.chosen_ref = bf16[3,2,128,256]{3,2,1,0:T(8,128)(2,1)S(1)} custom-call(s32[1]{0:T(128)S(6)} %copy.7.counts_ref, s32[1,6]{1,0:T(1,128)} %pairs_hbm.1, bf16[32,2,128,128]{3,2,1,0:T(8,128)(2,1)} %bitcast.12), custom_call_target="tpu_custom_call" | custom-call | bytes 786432 | tf_op jit(solution)/shard_map/pick/pallas_call | solution.py:187
  53.7 13.6 %all-to-all-done.1 = bf16[32,8,256]{2,1,0:T(8,128)(2,1)S(1)} async-done(((bf16[32,8,256]{2,1,0:T(8,128)(2,1)}), bf16[32,8,256]{2,1,0:T(8,128)(2,1)S(1)}, u32[]{:S(2)}, u32[]{:S(2)}) %all-to-all-start.1) | async-done | bytes 131104 | tf_op jit(solution)/shard_map/all_to_all | solution.py:186
  67.4 1.0 %blocks.1 = (f32[8,1,256]{2,1,0:T(1,128)}, f32[6,8,8,256]{3,2,1,0:T(8,128)}) custom-call(s32[1]{0:T(128)} %bitcast.band_ref, bf16[4,2,4,8,256]{4,3,2,1,0:T(8,128)(2,1)S(1)} %bitcast.11, bf16[3,2,128,256]{3,2,1,0:T(8,128)(2,1)S(1)} %pick.1.chosen_ref), custom_call_target="tpu_custom_call" | custom-call | tf_op jit(solution)/shard_map/blocks/pallas_call | solution.py:201
Async XLA Ops:
  26.0 41.4 %all-to-all-start.1 = ((bf16[32,8,256]{2,1,0:T(8,128)(2,1)}), bf16[32,8,256]{2,1,0:T(8,128)(2,1)S(1)}, u32[]{:S(2)}, u32[]{:S(2)}) async-start(bf16[32,8,256]{2,1,0:T(8,128)(2,1)} %bitcast.4), calls=%async_computation.1 | async-start | bytes 262144 | tf_op jit(solution)/shard_map/all_to_all | solution.py:186

commit v9 on v5

--- a/solution.py
+++ b/solution.py
@@ -13,7 +13,7 @@
 
 
 def gram_kernel(
-    base_ref, mom_hbm, pairs_hbm, evecs_hbm, peram_hbm, out_ref, chosen_ref,
+    base_ref, _, live_ref, mom_hbm, pairs_hbm, evecs_hbm, peram_hbm, out_ref, chosen_ref,
     evecs_ref, right_ref, mom_ref, pairs_ref, evecs_sems, small_sems, pick_sems,
 ):
     tcount, _, colours, sites, nvec = evecs_ref.shape
@@ -79,8 +79,12 @@
         for t in group:
             rotate(t)
             multiply(t)
-    for copy in picks:
+    for c, copy in enumerate(picks):
         copy.wait()
+
+        @pl.when(c >= live_ref[0])
+        def _():
+            chosen_ref[c] = jnp.zeros(chosen_ref.shape[1:], chosen_ref.dtype)
 
 
 def sum_kernel(parts_ref, out_ref):
@@ -89,15 +93,15 @@
         out_ref[band] = total
 
 
-def block_kernel(band_ref, counts_ref, parts_ref, chosen_ref, meson_hbm, out_hbm, total_ref, meson_ref, out_ref, sems):
-    cores, n_zh, _, rows, width = parts_ref.shape
+def block_kernel(band_ref, parts_ref, chosen_ref, meson_hbm, out_hbm, total_ref, meson_ref, out_ref, sems):
+    n_zh, cores, _, rows, width = parts_ref.shape
     moms = cores * n_zh
     slots = out_ref.shape[0]
     size = moms * rows
     nvec = width // 2
     for core in range(cores):
         for zh in range(n_zh):
-            total_ref[zh * cores + core] = jnp.sum(parts_ref[core, zh].astype(jnp.float32), axis=0)
+            total_ref[zh * cores + core] = jnp.sum(parts_ref[zh, core].astype(jnp.float32), axis=0)
     own = total_ref[band_ref[0]]
     for row in range(rows):
         meson_ref[row] = own[row : row + 1]
@@ -115,7 +119,7 @@
         prods = jnp.dot(both, right, preferred_element_type=jnp.float32)
         for q in range(2):
             c = 2 * pair + q
-            prod = jnp.where(c < counts_ref[0], prods[:, q * nvec : (q + 1) * nvec], 0.0)
+            prod = prods[:, q * nvec : (q + 1) * nvec]
             out_ref[c, :, :, :nvec] = prod[:size].reshape(rows, moms, nvec)
             out_ref[c, :, :, nvec:] = prod[size:].reshape(rows, moms, nvec)
             copies.append(pltpu.make_async_copy(out_ref.at[c], out_hbm.at[c], sems.at[c]))
@@ -137,12 +141,13 @@
     width = 2 * nvec
     place = (lax.axis_index("tm") * n_zl + lax.axis_index("z_lo")) * n_x + lax.axis_index("x")
     base = (place * piece_len).astype(jnp.int32)
+    band = (lax.axis_index("z_hi") * n_core + lax.axis_index("core")).astype(jnp.int32).reshape(1)
     smem = pl.BlockSpec(memory_space=pltpu.SMEM)
     vmem = pl.BlockSpec(memory_space=pltpu.VMEM)
     hbm = pl.BlockSpec(memory_space=pltpu.HBM)
     parts, chosen = pl.pallas_call(
         gram_kernel,
-        in_specs=[smem, hbm, hbm, hbm, hbm],
+        in_specs=[smem, smem, smem, hbm, hbm, hbm, hbm],
         out_specs=[vmem, vmem],
         out_shape=[
             jax.ShapeDtypeStruct((n_tm * n_x, n_zl, rows, width), jnp.bfloat16),
@@ -159,8 +164,10 @@
         ],
         compiler_params=pltpu.CompilerParams(vmem_limit_bytes=16 << 20),
         name="gram",
-    )(base.reshape(1), *(pltpu.with_memory_space_constraint(a, pltpu.HBM) for a in (mom, pairs, evecs, peram[0])))
+    )(base.reshape(1), band, counts, *(pltpu.with_memory_space_constraint(a, pltpu.HBM) for a in (mom, pairs, evecs, peram[0])))
+    parts = parts.reshape(n_tm * n_x, n_zl * rows, width)
     parts = lax.all_to_all(parts, ("x", "tm"), 0, 0, tiled=True)
+    parts = parts.reshape(n_tm * n_x, n_zl, rows, width)
     parts = pl.pallas_call(
         sum_kernel,
         in_specs=[vmem],
@@ -170,10 +177,10 @@
         name="total",
     )(parts)
     parts = parts.reshape(n_band * n_zl, rows, width)
-    parts = lax.all_to_all(parts, ("core", "z_hi", "z_lo"), 0, 0, tiled=True)
+    parts = lax.all_to_all(parts, ("z_hi", "core", "z_lo"), 0, 0, tiled=True)
     meson, blocks = pl.pallas_call(
         block_kernel,
-        in_specs=[smem, smem, vmem, vmem],
+        in_specs=[smem, vmem, vmem],
         out_specs=[hbm, hbm],
         out_shape=[
             jax.ShapeDtypeStruct((rows, 1, width), jnp.float32),
@@ -188,9 +195,8 @@
         compiler_params=pltpu.CompilerParams(vmem_limit_bytes=8 << 20),
         name="blocks",
     )(
-        (lax.axis_index("z_hi") * n_core + lax.axis_index("core")).astype(jnp.int32).reshape(1),
-        counts,
-        parts.reshape(n_core, n_zh, n_zl, rows, width),
+        band,
+        parts.reshape(n_zh, n_core, n_zl, rows, width),
         chosen,
     )
     return meson[None], blocks[None]

time: 69.1 us -> 69 us (level)
  blocking collectives: 21.7 us -> 62.8 us
  starting transfers between devices: 25.3 us -> 0 us
  waiting for transfers between devices: 15.7 us -> 0 us
    all_to_all x0 -> x1, blocking collectives: none -> 41.1 us  [per_device(): parts = lax.all_to_all(parts, ('z_hi', 'core', 'z_lo'), 0, 0, tiled=True)]
    all_to_all x1 -> x0, starting transfers between devices: 25.3 us -> none  [per_device(): parts = lax.all_to_all(parts, ('core', 'z_hi', 'z_lo'), 0, 0, tiled=True)]
    all_to_all x1 -> x0, waiting for transfers between devices: 15.7 us -> none  [per_device(): parts = lax.all_to_all(parts, ('core', 'z_hi', 'z_lo'), 0, 0, tiled=True)]
  transfers between devices with their start and end apart: 1 -> 0, of which waited for: 1 -> 0; matrix products, arithmetic and copies ran while one was open for 0% -> 0% of each run, Pallas kernels for 0% -> 0%
where the time goes in v9:
time: 69 us; the launch traced here: 68.2 us
  blocking collectives  62.8 us (91%)
  Pallas kernels  4.04 us (6%)
  between operations  1.3 us (2%)
    all_to_all x1, blocking collectives, per_device(): parts = lax.all_to_all(parts, ('z_hi', 'core', 'z_lo'), 0, 0, tiled=True)  41.1 us
    all_to_all x1, blocking collectives, per_device(): parts = lax.all_to_all(parts, ('x', 'tm'), 0, 0, tiled=True)  21.7 us
    pallas_call x1, Pallas kernels, per_device(): pl.pallas_call(gram_kernel, in_specs=[smem, smem, smem, hbm, hbm, hbm, hb...  2.96 us

profile of v9, /device:TPU:1, one launch (start us, length us, event | category | flops | bytes accessed | tf_op | source)
XLA Modules:
  0.0 68.2 jit_solution(12224880333031485050)
XLA Ops:
  1.3 3.0 %gram.1 = (bf16[32,4,8,256]{3,2,1,0:T(8,128)(2,1)S(1)}, bf16[6,2,128,128]{3,2,1,0:T(8,128)(2,1)S(1)}) custom-call(s32[1]{0:T(128)} %bitcast.1.base_ref, s32[1]{0:T(128)} %bitcast._.band_ref, s32[1]{0:T(128)S(6)} %copy.7.live_ref, s32[1,3]{1,0:T(1,128)} %mom_hbm.1, s32[1,6]{1,0:T(1,128)} %pairs_hbm.1, bf16[8,2,3,168,128]{4,3,2,1,0:T(8,128)(2,1)} %evecs_hbm.1, ...), custom_call_target="tpu_custom_call" | custom-call | tf_op jit(solution)/shard_map/gram/pallas_call | solution.py:148
  4.3 21.7 %all_to_all.10 = bf16[32,32,256]{2,1,0:T(8,128)(2,1)S(1)} all-to-all(bf16[32,32,256]{2,1,0:T(8,128)(2,1)S(1)} %bitcast.12), channel_id=1, replica_groups=mesh['tm'=8,'z_hi'=4,'core'=2,'z_lo'=4,'x'=4] {'x','tm'}, dimensions={0} | all-to-all | bytes 1048576 | tf_op jit(solution)/shard_map/all_to_all | solution.py:169
  26.0 0.1 total.1
  26.0 41.1 %all_to_all.11 = bf16[32,8,256]{2,1,0:T(8,128)(2,1)S(1)} all-to-all(bf16[32,8,256]{2,1,0:T(8,128)(2,1)S(1)} %bitcast.11), channel_id=1, replica_groups=mesh['tm'=8,'z_hi'=4,'core'=2,'z_lo'=4,'x'=4] {'z_hi','core','z_lo'}, dimensions={0} | all-to-all | bytes 262144 | tf_op jit(solution)/shard_map/all_to_all | solution.py:180
  67.2 1.0 %blocks.1 = (f32[8,1,256]{2,1,0:T(1,128)}, f32[6,8,8,256]{3,2,1,0:T(8,128)}) custom-call(s32[1]{0:T(128)} %bitcast._.band_ref, bf16[4,2,4,8,256]{4,3,2,1,0:T(8,128)(2,1)S(1)} %bitcast.10, bf16[6,2,128,128]{3,2,1,0:T(8,128)(2,1)S(1)} %get-tuple-element.7.chosen_ref), custom_call_target="tpu_custom_call" | custom-call | tf_op jit(solution)/shard_map/blocks/pallas_call | solution.py:181

commit v10 on v8

--- a/solution.py
+++ b/solution.py
@@ -46,11 +46,14 @@
     def multiply(t):
         right = right_ref[t].reshape(colours * sites, 2 * nvec)
         with_real, with_imag = (
-            lax.dot_general(
-                evecs_ref[t, part].reshape(colours * sites, nvec),
-                right,
-                (((0,), (0,)), ((), ())),
-                preferred_element_type=jnp.float32,
+            sum(
+                lax.dot_general(
+                    evecs_ref[t, part, colour],
+                    right_ref[t, colour],
+                    (((0,), (0,)), ((), ())),
+                    preferred_element_type=jnp.float32,
+                )
+                for colour in range(colours)
             )
             for part in range(2)
         )

time: 69.2 us -> 69.1 us (level)
  no operation moved by 1% of the time
where the time goes in v10:
time: 69.1 us; the launch traced here: 68.2 us
  starting transfers between devices  25.3 us (37%)
  blocking collectives  21.7 us (31%)
  waiting for transfers between devices  13.6 us (20%)
  Pallas kernels  6.25 us (9%)
  between operations  1.33 us (2%)
    all_to_all x1, starting transfers between devices, per_device(): parts = lax.all_to_all(parts, ('z_hi', 'core', 'z_lo'), 0, 0, tiled=True)  25.3 us
    all_to_all x1, blocking collectives, per_device(): parts = lax.all_to_all(parts, ('x', 'tm'), 0, 0, tiled=True)  21.7 us
    all_to_all x1, waiting for transfers between devices, per_device(): parts = lax.all_to_all(parts, ('z_hi', 'core', 'z_lo'), 0, 0, tiled=True)  13.6 us
    pallas_call x1, Pallas kernels, per_device(): pl.pallas_call(gram_kernel, in_specs=[smem, hbm, hbm], out_specs=vmem, ou...  2.73 us
    pallas_call x1, Pallas kernels, per_device(): pl.pallas_call(pick_kernel, in_specs=[smem, hbm, hbm], out_specs=vmem, ou...  1.73 us
  transfers between devices with their start and end apart: 1, of which 1 were waited for; matrix products, arithmetic and copies ran while one was open for 0% of the time, Pallas kernels for 3%

profile of v10, /device:TPU:1, one launch (start us, length us, event | category | flops | bytes accessed | tf_op | source)
XLA Modules:
  0.0 68.2 jit_solution(5211708450208781862)
XLA Ops:
  0.6 2.7 %gram.1 = bf16[32,4,8,256]{3,2,1,0:T(8,128)(2,1)S(1)} custom-call(s32[1]{0:T(128)} %bitcast.1.base_ref, s32[1,3]{1,0:T(1,128)} %mom_hbm.1, bf16[8,2,3,168,128]{4,3,2,1,0:T(8,128)(2,1)} %evecs_hbm.1), custom_call_target="tpu_custom_call" | custom-call | tf_op jit(solution)/shard_map/gram/pallas_call | solution.py:161
  3.4 21.7 %all_to_all.10 = bf16[32,32,256]{2,1,0:T(8,128)(2,1)S(1)} all-to-all(bf16[32,32,256]{2,1,0:T(8,128)(2,1)S(1)} %bitcast.10), channel_id=1, replica_groups=mesh['tm'=8,'z_hi'=4,'core'=2,'z_lo'=4,'x'=4] {'x','tm'}, dimensions={0} | all-to-all | bytes 1048576 | tf_op jit(solution)/shard_map/all_to_all | solution.py:177
  25.1 0.8 %total.1 = bf16[8,4,8,256]{3,2,1,0:T(8,128)(2,1)} custom-call(bf16[32,4,8,256]{3,2,1,0:T(8,128)(2,1)S(1)} %bitcast.9), custom_call_target="tpu_custom_call" | custom-call | tf_op jit(solution)/shard_map/total/pallas_call | solution.py:179
  25.9 25.3 %all-to-all-start.1 = ((bf16[32,8,256]{2,1,0:T(8,128)(2,1)}), bf16[32,8,256]{2,1,0:T(8,128)(2,1)S(1)}, u32[]{:S(2)}, u32[]{:S(2)}) async-start(bf16[32,8,256]{2,1,0:T(8,128)(2,1)} %bitcast.4), calls=%async_computation.1 | async-start | bytes 262144 | tf_op jit(solution)/shard_map/all_to_all | solution.py:189
  51.9 1.7 %pick.1.chosen_ref = bf16[3,2,128,256]{3,2,1,0:T(8,128)(2,1)S(1)} custom-call(s32[1]{0:T(128)S(6)} %copy.7.counts_ref, s32[1,6]{1,0:T(1,128)} %pairs_hbm.1, bf16[32,2,128,128]{3,2,1,0:T(8,128)(2,1)} %bitcast.12), custom_call_target="tpu_custom_call" | custom-call | bytes 786432 | tf_op jit(solution)/shard_map/pick/pallas_call | solution.py:190
  53.6 13.6 %all-to-all-done.1 = bf16[32,8,256]{2,1,0:T(8,128)(2,1)S(1)} async-done(((bf16[32,8,256]{2,1,0:T(8,128)(2,1)}), bf16[32,8,256]{2,1,0:T(8,128)(2,1)S(1)}, u32[]{:S(2)}, u32[]{:S(2)}) %all-to-all-start.1) | async-done | bytes 131104 | tf_op jit(solution)/shard_map/all_to_all | solution.py:189
  67.3 1.0 %blocks.1 = (f32[8,1,256]{2,1,0:T(1,128)}, f32[6,8,8,256]{3,2,1,0:T(8,128)}) custom-call(s32[1]{0:T(128)} %bitcast.band_ref, bf16[4,2,4,8,256]{4,3,2,1,0:T(8,128)(2,1)S(1)} %bitcast.11, bf16[3,2,128,256]{3,2,1,0:T(8,128)(2,1)S(1)} %pick.1.chosen_ref), custom_call_target="tpu_custom_call" | custom-call | tf_op jit(solution)/shard_map/blocks/pallas_call | solution.py:204
Async XLA Ops:
  25.9 41.4 %all-to-all-start.1 = ((bf16[32,8,256]{2,1,0:T(8,128)(2,1)}), bf16[32,8,256]{2,1,0:T(8,128)(2,1)S(1)}, u32[]{:S(2)}, u32[]{:S(2)}) async-start(bf16[32,8,256]{2,1,0:T(8,128)(2,1)} %bitcast.4), calls=%async_computation.1 | async-start | bytes 262144 | tf_op jit(solution)/shard_map/all_to_all | solution.py:189

commit v11 on v8

--- a/solution.py
+++ b/solution.py
@@ -72,12 +72,12 @@
 
 
 def sum_kernel(parts_ref, out_hbm, total_ref, sems):
-    total_ref[...] = jnp.sum(parts_ref[...].astype(jnp.float32), axis=0).astype(jnp.bfloat16)
-    copies = [
-        pltpu.make_async_copy(total_ref, out_hbm.at[band], sems.at[band]) for band in range(out_hbm.shape[0])
-    ]
-    for copy in copies:
-        copy.start()
+    copies = []
+    for zl in range(total_ref.shape[0]):
+        total_ref[zl] = jnp.sum(parts_ref[:, zl].astype(jnp.float32), axis=0).astype(jnp.bfloat16)
+        for band in range(out_hbm.shape[0]):
+            copies.append(pltpu.make_async_copy(total_ref.at[zl], out_hbm.at[band, zl], sems.at[band, zl]))
+            copies[-1].start()
     for copy in copies:
         copy.wait()
 
@@ -178,7 +178,7 @@
         in_specs=[vmem],
         out_specs=hbm,
         out_shape=jax.ShapeDtypeStruct((n_band, n_zl, rows, width), jnp.bfloat16),
-        scratch_shapes=[pltpu.VMEM((n_zl, rows, width), jnp.bfloat16), pltpu.SemaphoreType.DMA((n_band,))],
+        scratch_shapes=[pltpu.VMEM((n_zl, rows, width), jnp.bfloat16), pltpu.SemaphoreType.DMA((n_band, n_zl))],
         compiler_params=pltpu.CompilerParams(vmem_limit_bytes=8 << 20),
         name="total",
     )(parts)

time: 69.2 us -> 69.5 us (level)
  no operation moved by 1% of the time
where the time goes in v11:
time: 69.5 us; the launch traced here: 68.6 us
  starting transfers between devices  25.3 us (36%)
  blocking collectives  21.7 us (31%)
  waiting for transfers between devices  13.6 us (20%)
  Pallas kernels  6.6 us (9%)
  between operations  1.33 us (2%)
    all_to_all x1, starting transfers between devices, per_device(): parts = lax.all_to_all(parts, ('z_hi', 'core', 'z_lo'), 0, 0, tiled=True)  25.3 us
    all_to_all x1, blocking collectives, per_device(): parts = lax.all_to_all(parts, ('x', 'tm'), 0, 0, tiled=True)  21.7 us
    all_to_all x1, waiting for transfers between devices, per_device(): parts = lax.all_to_all(parts, ('z_hi', 'core', 'z_lo'), 0, 0, tiled=True)  13.6 us
    pallas_call x1, Pallas kernels, per_device(): pl.pallas_call(gram_kernel, in_specs=[smem, hbm, hbm], out_specs=vmem, ou...  2.84 us
    pallas_call x1, Pallas kernels, per_device(): pl.pallas_call(pick_kernel, in_specs=[smem, hbm, hbm], out_specs=vmem, ou...  1.74 us
  transfers between devices with their start and end apart: 1, of which 1 were waited for; matrix products, arithmetic and copies ran while one was open for 0% of the time, Pallas kernels for 3%

profile of v11, /device:TPU:1, one launch (start us, length us, event | category | flops | bytes accessed | tf_op | source)
XLA Modules:
  0.0 68.6 jit_solution(3595639040831291387)
XLA Ops:
  0.6 2.8 %gram.1 = bf16[32,4,8,256]{3,2,1,0:T(8,128)(2,1)S(1)} custom-call(s32[1]{0:T(128)} %bitcast.1.base_ref, s32[1,3]{1,0:T(1,128)} %mom_hbm.1, bf16[8,2,3,168,128]{4,3,2,1,0:T(8,128)(2,1)} %evecs_hbm.1), custom_call_target="tpu_custom_call" | custom-call | tf_op jit(solution)/shard_map/gram/pallas_call | solution.py:158
  3.5 21.7 %all_to_all.10 = bf16[32,32,256]{2,1,0:T(8,128)(2,1)S(1)} all-to-all(bf16[32,32,256]{2,1,0:T(8,128)(2,1)S(1)} %bitcast.10), channel_id=1, replica_groups=mesh['tm'=8,'z_hi'=4,'core'=2,'z_lo'=4,'x'=4] {'x','tm'}, dimensions={0} | all-to-all | bytes 1048576 | tf_op jit(solution)/shard_map/all_to_all | solution.py:174
  25.2 1.0 %total.1 = bf16[8,4,8,256]{3,2,1,0:T(8,128)(2,1)} custom-call(bf16[32,4,8,256]{3,2,1,0:T(8,128)(2,1)S(1)} %bitcast.9), custom_call_target="tpu_custom_call" | custom-call | tf_op jit(solution)/shard_map/total/pallas_call | solution.py:176
  26.2 25.3 %all-to-all-start.1 = ((bf16[32,8,256]{2,1,0:T(8,128)(2,1)}), bf16[32,8,256]{2,1,0:T(8,128)(2,1)S(1)}, u32[]{:S(2)}, u32[]{:S(2)}) async-start(bf16[32,8,256]{2,1,0:T(8,128)(2,1)} %bitcast.4), calls=%async_computation.1 | async-start | bytes 262144 | tf_op jit(solution)/shard_map/all_to_all | solution.py:186
  52.2 1.7 %pick.1.chosen_ref = bf16[3,2,128,256]{3,2,1,0:T(8,128)(2,1)S(1)} custom-call(s32[1]{0:T(128)S(6)} %copy.7.counts_ref, s32[1,6]{1,0:T(1,128)} %pairs_hbm.1, bf16[32,2,128,128]{3,2,1,0:T(8,128)(2,1)} %bitcast.12), custom_call_target="tpu_custom_call" | custom-call | bytes 786432 | tf_op jit(solution)/shard_map/pick/pallas_call | solution.py:187
  54.0 13.6 %all-to-all-done.1 = bf16[32,8,256]{2,1,0:T(8,128)(2,1)S(1)} async-done(((bf16[32,8,256]{2,1,0:T(8,128)(2,1)}), bf16[32,8,256]{2,1,0:T(8,128)(2,1)S(1)}, u32[]{:S(2)}, u32[]{:S(2)}) %all-to-all-start.1) | async-done | bytes 131104 | tf_op jit(solution)/shard_map/all_to_all | solution.py:186
  67.6 1.0 %blocks.1 = (f32[8,1,256]{2,1,0:T(1,128)}, f32[6,8,8,256]{3,2,1,0:T(8,128)}) custom-call(s32[1]{0:T(128)} %bitcast.band_ref, bf16[4,2,4,8,256]{4,3,2,1,0:T(8,128)(2,1)S(1)} %bitcast.11, bf16[3,2,128,256]{3,2,1,0:T(8,128)(2,1)S(1)} %pick.1.chosen_ref), custom_call_target="tpu_custom_call" | custom-call | tf_op jit(solution)/shard_map/blocks/pallas_call | solution.py:201
Async XLA Ops:
  26.2 41.4 %all-to-all-start.1 = ((bf16[32,8,256]{2,1,0:T(8,128)(2,1)}), bf16[32,8,256]{2,1,0:T(8,128)(2,1)S(1)}, u32[]{:S(2)}, u32[]{:S(2)}) async-start(bf16[32,8,256]{2,1,0:T(8,128)(2,1)} %bitcast.4), calls=%async_computation.1 | async-start | bytes 262144 | tf_op jit(solution)/shard_map/all_to_all | solution.py:186
